TPU v7x, 256 devices: a whole 4x4x8 slice. The times are simulated.
256 devices in a mesh: leaf: 256 (over z, x, y, core).
Axes of the slice: x: 4, y: 4, z: 8, core: 2. Of those that a mesh axis runs over, the one named last changes fastest.
Arguments:
- leaf_inverse: float32 [2048, 256, 256], P('leaf'), may hold values from -200 to 200, as said below
- node_bases: float32 [524288, 5, 128], P('leaf'), may hold values from -6 to 6
- right_sides: float32 [524288, 128], P('leaf'), may hold values from -6 to 6
Outputs:
- solution: float32 [524288, 128], P('leaf')
- log_determinant: float32 [], replicated
Inputs may be any that keep to these rules, and one draw needn't show every extreme that they name: Each leaf block of leaf_inverse is symmetric positive definite.
All inputs are finite; a program needn't handle non-finite values.
Results may differ from a plain program's by a relative error of at most 0.0003.
Values sent between devices are 32-bit elements; how exact they have to be, the bound alone decides.
A program may use at most 128 MiB of HBM per device.

v0:
```python
import jax
import jax.numpy as jnp
from jax import lax
from jax.sharding import PartitionSpec as P


def swapped(value, axis, bit):
    mask = 2**bit
    pairs = [(source, source ^ mask) for source in range(lax.axis_size(axis))]
    return lax.ppermute(value, axis, pairs)


def cholesky_solve(factor, targets):
    middle = lax.linalg.triangular_solve(factor, targets, left_side=True, lower=True)
    return lax.linalg.triangular_solve(factor, middle, left_side=True, lower=True, transpose_a=True)


def paired_sums(partial_value, bit_count):
    for bit_index in range(bit_count):
        partial_value = partial_value + swapped(partial_value, "leaf", bit_index)
    return partial_value


def body(leaf_inverse, node_bases, right_sides):
    row_count = right_sides.shape[0]
    leaf_size = leaf_inverse.shape[1]
    level_count = node_bases.shape[1]
    rank_size = node_bases.shape[2]
    columns = jnp.concatenate(
        [node_bases.reshape(row_count, level_count * rank_size), right_sides], axis=1
    )
    blocks = columns.reshape(leaf_inverse.shape[0], leaf_size, -1)
    current = jnp.einsum("lij,ljc->lic", leaf_inverse, blocks, precision=lax.Precision.HIGHEST)
    current = current.reshape(row_count, -1)
    depth = lax.axis_size("leaf").bit_length() - 1
    log_share = jnp.zeros((), jnp.float32)
    for level_index in range(level_count):
        bit_count = depth - (level_count - 1 - level_index)
        basis = node_bases[:, level_index, :]
        partial_value = jnp.einsum("ir,ic->rc", basis, current, precision=lax.Precision.HIGHEST)
        summed = paired_sums(partial_value, bit_count)
        capacity = jnp.eye(rank_size, dtype=jnp.float32) + summed[:, :rank_size]
        factor = jnp.linalg.cholesky(capacity)
        weights = cholesky_solve(factor, summed[:, rank_size:])
        update = jnp.dot(
            current[:, :rank_size],
            weights,
            precision=lax.Precision.HIGHEST,
            preferred_element_type=jnp.float32,
        )
        current = current[:, rank_size:] - update
        log_share = log_share + 2.0 * jnp.sum(jnp.log(jnp.diagonal(factor))) / 2**bit_count
    total_log = lax.psum(log_share, "leaf")
    return (current, total_log / (rank_size * (2**level_count - 1)))


def solution(mesh):
    return jax.shard_map(
        body,
        mesh=mesh,
        in_specs=(P("leaf", None, None), P("leaf", None, None), P("leaf", None)),
        out_specs=(P("leaf", None), P()),
        check_vma=False,
    )
```

profile of v0, /device:TPU:1, one launch (start us, length us, event | category | flops | bytes accessed | tf_op | source)
XLA Modules:
  0.0 513.7 jit_solution(3455252941334297169)
XLA Ops:
  0.6 8.7 %copy.18 = f32[2048,5,128]{2,1,0:T(8,128)} copy(f32[2048,5,128]{2,0,1:T(8,128)} %param.5) | data formatting | bytes 10485760 | tf_op jit(solution)/shard_map/concatenate | solution.py:29
  9.4 8.3 %reshape.73 = f32[8,256,640]{2,1,0:T(8,128)} reshape(f32[2048,5,128]{2,1,0:T(8,128)} %copy.18) | data formatting | bytes 10485760 | tf_op jit(solution)/shard_map/concatenate | solution.py:29
  17.7 8.4 %fusion = f32[8,768,256]{1,2,0:T(8,128)S(1)} fusion(f32[8,256,256]{2,1,0:T(8,128)S(1)} %copy-done, f32[8,256,128]{2,1,0:T(8,128)S(1)} %bitcast.104, f32[8,256,640]{2,1,0:T(8,128)} %reshape.73), kind=kOutput, calls=%fused_computation.5 | convolution fusion | flops 4833411072 | bytes 14680064 | tf_op jit(solution)/shard_map/lij,ljc->lic/dot_general | solution.py:33
  26.1 12.1 %convolution_bitcast_fusion = f32[128,768]{0,1:T(8,128)S(1)} fusion(f32[2048,768]{1,0:T(8,128)S(1)} %bitcast.102, f32[2048,5,128]{2,0,1:T(8,128)} %param.5), kind=kOutput, calls=%fused_computation.14 | convolution fusion | flops 2415919104 | bytes 7733248 | tf_op jit(solution)/shard_map/ir,ic->rc/dot_general | solution.py:40
  43.1 10.3 %collective-permute-done.1 = f32[128,768]{0,1:T(8,128)S(1)} collective-permute-done((f32[128,768]{0,1:T(8,128)S(1)}, f32[128,768]{0,1:T(8,128)S(1)}, u32[]{:S(2)}, u32[]{:S(2)}) %collective-permute-start.1) | collective-permute-done | bytes 393248 | tf_op jit(solution)/shard_map/ppermute | solution.py:10
  54.7 9.7 %collective-permute-done.2 = f32[128,768]{0,1:T(8,128)S(1)} collective-permute-done((f32[128,768]{0,1:T(8,128)S(1)}, f32[128,768]{0,1:T(8,128)S(1)}, u32[]{:S(2)}, u32[]{:S(2)}) %collective-permute-start.2) | collective-permute-done | bytes 393248 | tf_op jit(solution)/shard_map/ppermute | solution.py:10
  65.0 8.6 %collective-permute-done.3 = f32[128,768]{0,1:T(8,128)S(1)} collective-permute-done((f32[128,768]{0,1:T(8,128)S(1)}, f32[128,768]{0,1:T(8,128)S(1)}, u32[]{:S(2)}, u32[]{:S(2)}) %collective-permute-start.3) | collective-permute-done | bytes 393248 | tf_op jit(solution)/shard_map/ppermute | solution.py:10
  73.8 11.7 %cholesky.89 = f32[128,128]{1,0:T(8,128)S(1)} custom-call(f32[128,128]{1,0:T(8,128)S(1)} %fusion.48), custom_call_target="Cholesky" | custom-call | tf_op jit(solution)/shard_map/jit(cholesky)/cholesky | solution.py:43
  86.8 9.8 %custom-call.27 = f32[1,128,128]{1,2,0:T(8,128)S(1)} custom-call(f32[1,128,128]{2,1,0:T(8,128)S(1)} %get-tuple-element.11), custom_call_target="InvertDiagBlocksLowerTriangular" | custom-call | tf_op jit(solution)/shard_map/triangular_solve | solution.py:15
  97.6 6.8 %slice_subtract_fusion = f32[2048,640]{1,0:T(8,128)S(1)} fusion(f32[2048,768]{1,0:T(8,128)} %bitcast.103, f32[128,640]{1,0:T(8,128)S(1)} %fusion.45), kind=kOutput, calls=%fused_computation.9 | convolution fusion | flops 2014576640 | bytes 11862016 | tf_op jit(solution)/shard_map/dot_general | solution.py:45
  104.4 10.4 %convolution_bitcast_fusion.1 = f32[128,640]{0,1:T(8,128)S(1)} fusion(f32[2048,640]{1,0:T(8,128)S(1)} %slice_subtract_fusion, f32[2048,5,128]{2,0,1:T(8,128)} %param.5), kind=kOutput, calls=%fused_computation.15 | convolution fusion | flops 2013265920 | bytes 6619136 | tf_op jit(solution)/shard_map/ir,ic->rc/dot_general | solution.py:40
  119.8 8.3 %collective-permute-done.5 = f32[128,640]{0,1:T(8,128)S(1)} collective-permute-done((f32[128,640]{0,1:T(8,128)S(1)}, f32[128,640]{0,1:T(8,128)S(1)}, u32[]{:S(2)}, u32[]{:S(2)}) %collective-permute-start.5) | collective-permute-done | bytes 327712 | tf_op jit(solution)/shard_map/ppermute | solution.py:10
  129.6 8.3 %collective-permute-done.6 = f32[128,640]{0,1:T(8,128)S(1)} collective-permute-done((f32[128,640]{0,1:T(8,128)S(1)}, f32[128,640]{0,1:T(8,128)S(1)}, u32[]{:S(2)}, u32[]{:S(2)}) %collective-permute-start.6) | collective-permute-done | bytes 327712 | tf_op jit(solution)/shard_map/ppermute | solution.py:10
  138.1 7.2 %collective-permute-done.7 = f32[128,640]{0,1:T(8,128)S(1)} collective-permute-done((f32[128,640]{0,1:T(8,128)S(1)}, f32[128,640]{0,1:T(8,128)S(1)}, u32[]{:S(2)}, u32[]{:S(2)}) %collective-permute-start.7) | collective-permute-done | bytes 327712 | tf_op jit(solution)/shard_map/ppermute | solution.py:10
  146.5 6.8 %collective-permute-done.8 = f32[128,640]{0,1:T(8,128)S(1)} collective-permute-done((f32[128,640]{0,1:T(8,128)S(1)}, f32[128,640]{0,1:T(8,128)S(1)}, u32[]{:S(2)}, u32[]{:S(2)}) %collective-permute-start.8) | collective-permute-done | bytes 327712 | tf_op jit(solution)/shard_map/ppermute | solution.py:10
  153.4 11.7 %cholesky.100 = f32[128,128]{1,0:T(8,128)S(1)} custom-call(f32[128,128]{1,0:T(8,128)S(1)} %fusion.44), custom_call_target="Cholesky" | custom-call | tf_op jit(solution)/shard_map/jit(cholesky)/cholesky | solution.py:43
  166.5 9.8 %custom-call.28 = f32[1,128,128]{1,2,0:T(8,128)S(1)} custom-call(f32[1,128,128]{2,1,0:T(8,128)S(1)} %get-tuple-element.9), custom_call_target="InvertDiagBlocksLowerTriangular" | custom-call | tf_op jit(solution)/shard_map/triangular_solve | solution.py:15
  177.1 7.4 %slice_subtract_fusion.1 = f32[2048,512]{1,0:T(8,128)S(1)} fusion(f32[2048,640]{1,0:T(8,128)} %copy-done.2, f32[128,512]{1,0:T(8,128)S(1)} %fusion.41), kind=kOutput, calls=%fused_computation.10 | convolution fusion | flops 1611661312 | bytes 9699328 | tf_op jit(solution)/shard_map/dot_general | solution.py:45
  186.5 8.0 %convolution_bitcast_fusion.2 = f32[128,512]{0,1:T(8,128)S(1)} fusion(f32[2048,512]{1,0:T(8,128)S(1)} %slice_subtract_fusion.1, f32[2048,5,128]{2,0,1:T(8,128)} %param.5), kind=kOutput, calls=%fused_computation.16 | convolution fusion | flops 1610612736 | bytes 5505024 | tf_op jit(solution)/shard_map/ir,ic->rc/dot_general | solution.py:40
  200.2 6.9 %collective-permute-done.10 = f32[128,512]{0,1:T(8,128)S(1)} collective-permute-done((f32[128,512]{0,1:T(8,128)S(1)}, f32[128,512]{0,1:T(8,128)S(1)}, u32[]{:S(2)}, u32[]{:S(2)}) %collective-permute-start.10) | collective-permute-done | bytes 262176 | tf_op jit(solution)/shard_map/ppermute | solution.py:10
  208.8 6.6 %collective-permute-done.11 = f32[128,512]{0,1:T(8,128)S(1)} collective-permute-done((f32[128,512]{0,1:T(8,128)S(1)}, f32[128,512]{0,1:T(8,128)S(1)}, u32[]{:S(2)}, u32[]{:S(2)}) %collective-permute-start.11) | collective-permute-done | bytes 262176 | tf_op jit(solution)/shard_map/ppermute | solution.py:10
  215.5 5.8 %collective-permute-done.12 = f32[128,512]{0,1:T(8,128)S(1)} collective-permute-done((f32[128,512]{0,1:T(8,128)S(1)}, f32[128,512]{0,1:T(8,128)S(1)}, u32[]{:S(2)}, u32[]{:S(2)}) %collective-permute-start.12) | collective-permute-done | bytes 262176 | tf_op jit(solution)/shard_map/ppermute | solution.py:10
  233.8 11.7 %cholesky.111 = f32[128,128]{1,0:T(8,128)S(1)} custom-call(f32[128,128]{1,0:T(8,128)S(1)} %fusion.40), custom_call_target="Cholesky" | custom-call | tf_op jit(solution)/shard_map/jit(cholesky)/cholesky | solution.py:43
  246.9 9.8 %custom-call.29 = f32[1,128,128]{1,2,0:T(8,128)S(1)} custom-call(f32[1,128,128]{2,1,0:T(8,128)S(1)} %get-tuple-element.7), custom_call_target="InvertDiagBlocksLowerTriangular" | custom-call | tf_op jit(solution)/shard_map/triangular_solve | solution.py:15
  264.2 6.7 %convolution_bitcast_fusion.3 = f32[128,384]{0,1:T(8,128)S(1)} fusion(f32[2048,384]{1,0:T(8,128)S(1)} %slice_subtract_fusion.2, f32[2048,5,128]{2,0,1:T(8,128)} %param.5), kind=kOutput, calls=%fused_computation.17 | convolution fusion | flops 1207959552 | bytes 4390912 | tf_op jit(solution)/shard_map/ir,ic->rc/dot_general | solution.py:40
  312.9 11.7 %cholesky.122 = f32[128,128]{1,0:T(8,128)S(1)} custom-call(f32[128,128]{1,0:T(8,128)S(1)} %fusion.36), custom_call_target="Cholesky" | custom-call | tf_op jit(solution)/shard_map/jit(cholesky)/cholesky | solution.py:43
  326.0 9.8 %custom-call.30 = f32[1,128,128]{1,2,0:T(8,128)S(1)} custom-call(f32[1,128,128]{2,1,0:T(8,128)S(1)} %get-tuple-element.5), custom_call_target="InvertDiagBlocksLowerTriangular" | custom-call | tf_op jit(solution)/shard_map/triangular_solve | solution.py:15
  345.7 8.6 %collective-permute-start.22 = (f32[128,256]{0,1:T(8,128)S(1)}, f32[128,256]{0,1:T(8,128)S(1)}, u32[]{:S(2)}, u32[]{:S(2)}) collective-permute-start(f32[128,256]{0,1:T(8,128)S(1)} %convolution_bitcast_fusion.4), channel_id=1, source_target_pairs={{0,1},{1,0},{2,3},{3,2},{4,5},{5,4},{6,7},{7,6},{8,9},{9,8},{10,11... | collective-permute-start | bytes 393224 | tf_op jit(solution)/shard_map/ppermute | solution.py:10
  387.4 5.7 %collective-permute-start.29 = (f32[128,256]{0,1:T(8,128)S(1)}, f32[128,256]{0,1:T(8,128)S(1)}, u32[]{:S(2)}, u32[]{:S(2)}) collective-permute-start(f32[128,256]{0,1:T(8,128)S(1)} %add.190), channel_id=1, source_target_pairs={{0,128},{1,129},{2,130},{3,131},{4,132},{5,133},{6,134},{7,135},{8... | collective-permute-start | bytes 393224 | tf_op jit(solution)/shard_map/ppermute | solution.py:10
  397.1 11.7 %cholesky.133 = f32[128,128]{1,0:T(8,128)S(1)} custom-call(f32[128,128]{1,0:T(8,128)S(1)} %fusion.32), custom_call_target="Cholesky" | custom-call | tf_op jit(solution)/shard_map/jit(cholesky)/cholesky | solution.py:43
  412.6 85.2 %psum.7 = f32[]{:T(128)} all-reduce(f32[]{:T(128)S(6)} %add.196), channel_id=1, replica_groups=mesh['leaf'=256] {'leaf'}, use_global_device_ids=true, to_apply=%region_7.9 | all-reduce | flops 1 | bytes 8 | tf_op jit(solution)/shard_map/psum | solution.py:53
  497.8 9.8 %custom-call.31 = f32[1,128,128]{1,2,0:T(8,128)S(1)} custom-call(f32[1,128,128]{2,1,0:T(8,128)S(1)} %get-tuple-element.3), custom_call_target="InvertDiagBlocksLowerTriangular" | custom-call | tf_op jit(solution)/shard_map/triangular_solve | solution.py:15
  (147 shorter events, 144.5 us)
Async XLA Ops:
  38.3 4.6 collective-permute-start
  43.0 10.4 %collective-permute-start.1 = (f32[128,768]{0,1:T(8,128)S(1)}, f32[128,768]{0,1:T(8,128)S(1)}, u32[]{:S(2)}, u32[]{:S(2)}) collective-permute-start(f32[128,768]{0,1:T(8,128)S(1)} %add.158), channel_id=1, source_target_pairs={{0,2},{1,3},{2,0},{3,1},{4,6},{5,7},{6,4},{7,5},{8,10},{9,11},{10,... | collective-permute-start | bytes 1179656 | tf_op jit(solution)/shard_map/ppermute | solution.py:10
  53.4 11.0 %collective-permute-start.2 = (f32[128,768]{0,1:T(8,128)S(1)}, f32[128,768]{0,1:T(8,128)S(1)}, u32[]{:S(2)}, u32[]{:S(2)}) collective-permute-start(f32[128,768]{0,1:T(8,128)S(1)} %add.159), channel_id=1, source_target_pairs={{0,4},{1,5},{2,6},{3,7},{4,0},{5,1},{6,2},{7,3},{8,12},{9,13},{10,... | collective-permute-start | bytes 1179656 | tf_op jit(solution)/shard_map/ppermute | solution.py:10
  64.5 9.1 %collective-permute-start.3 = (f32[128,768]{0,1:T(8,128)S(1)}, f32[128,768]{0,1:T(8,128)S(1)}, u32[]{:S(2)}, u32[]{:S(2)}) collective-permute-start(f32[128,768]{0,1:T(8,128)S(1)} %add.160), channel_id=1, source_target_pairs={{0,8},{1,9},{2,10},{3,11},{4,12},{5,13},{6,14},{7,15},{8,0},{9,1},... | collective-permute-start | bytes 1179656 | tf_op jit(solution)/shard_map/ppermute | solution.py:10
  104.4 40.9 %copy-start.2 = (f32[2048,640]{1,0:T(8,128)}, f32[2048,640]{1,0:T(8,128)S(1)}, u32[]{:S(2)}) copy-start(f32[2048,640]{1,0:T(8,128)S(1)} %slice_subtract_fusion) | copy-start | bytes 15728644
  114.8 4.3 collective-permute-start.4
  119.1 9.0 %collective-permute-start.5 = (f32[128,640]{0,1:T(8,128)S(1)}, f32[128,640]{0,1:T(8,128)S(1)}, u32[]{:S(2)}, u32[]{:S(2)}) collective-permute-start(f32[128,640]{0,1:T(8,128)S(1)} %add.163), channel_id=1, source_target_pairs={{0,2},{1,3},{2,0},{3,1},{4,6},{5,7},{6,4},{7,5},{8,10},{9,11},{10,... | collective-permute-start | bytes 983048 | tf_op jit(solution)/shard_map/ppermute | solution.py:10
  128.1 9.8 %collective-permute-start.6 = (f32[128,640]{0,1:T(8,128)S(1)}, f32[128,640]{0,1:T(8,128)S(1)}, u32[]{:S(2)}, u32[]{:S(2)}) collective-permute-start(f32[128,640]{0,1:T(8,128)S(1)} %add.164), channel_id=1, source_target_pairs={{0,4},{1,5},{2,6},{3,7},{4,0},{5,1},{6,2},{7,3},{8,12},{9,13},{10,... | collective-permute-start | bytes 983048 | tf_op jit(solution)/shard_map/ppermute | solution.py:10
  138.0 7.3 %collective-permute-start.7 = (f32[128,640]{0,1:T(8,128)S(1)}, f32[128,640]{0,1:T(8,128)S(1)}, u32[]{:S(2)}, u32[]{:S(2)}) collective-permute-start(f32[128,640]{0,1:T(8,128)S(1)} %add.165), channel_id=1, source_target_pairs={{0,8},{1,9},{2,10},{3,11},{4,12},{5,13},{6,14},{7,15},{8,0},{9,1},... | collective-permute-start | bytes 983048 | tf_op jit(solution)/shard_map/ppermute | solution.py:10
  145.3 7.9 %collective-permute-start.8 = (f32[128,640]{0,1:T(8,128)S(1)}, f32[128,640]{0,1:T(8,128)S(1)}, u32[]{:S(2)}, u32[]{:S(2)}) collective-permute-start(f32[128,640]{0,1:T(8,128)S(1)} %add.166), channel_id=1, source_target_pairs={{0,16},{1,17},{2,18},{3,19},{4,20},{5,21},{6,22},{7,23},{8,24},{9,... | collective-permute-start | bytes 983048 | tf_op jit(solution)/shard_map/ppermute | solution.py:10
  194.5 5.1 collective-permute-start.9
  199.6 7.6 %collective-permute-start.10 = (f32[128,512]{0,1:T(8,128)S(1)}, f32[128,512]{0,1:T(8,128)S(1)}, u32[]{:S(2)}, u32[]{:S(2)}) collective-permute-start(f32[128,512]{0,1:T(8,128)S(1)} %add.169), channel_id=1, source_target_pairs={{0,2},{1,3},{2,0},{3,1},{4,6},{5,7},{6,4},{7,5},{8,10},{9,11},{10,... | collective-permute-start | bytes 786440 | tf_op jit(solution)/shard_map/ppermute | solution.py:10
  207.2 8.2 %collective-permute-start.11 = (f32[128,512]{0,1:T(8,128)S(1)}, f32[128,512]{0,1:T(8,128)S(1)}, u32[]{:S(2)}, u32[]{:S(2)}) collective-permute-start(f32[128,512]{0,1:T(8,128)S(1)} %add.170), channel_id=1, source_target_pairs={{0,4},{1,5},{2,6},{3,7},{4,0},{5,1},{6,2},{7,3},{8,12},{9,13},{10,... | collective-permute-start | bytes 786440 | tf_op jit(solution)/shard_map/ppermute | solution.py:10
  215.4 5.9 %collective-permute-start.12 = (f32[128,512]{0,1:T(8,128)S(1)}, f32[128,512]{0,1:T(8,128)S(1)}, u32[]{:S(2)}, u32[]{:S(2)}) collective-permute-start(f32[128,512]{0,1:T(8,128)S(1)} %add.171), channel_id=1, source_target_pairs={{0,8},{1,9},{2,10},{3,11},{4,12},{5,13},{6,14},{7,15},{8,0},{9,1},... | collective-permute-start | bytes 786440 | tf_op jit(solution)/shard_map/ppermute | solution.py:10
  221.3 6.8 %collective-permute-start.13 = (f32[128,512]{0,1:T(8,128)S(1)}, f32[128,512]{0,1:T(8,128)S(1)}, u32[]{:S(2)}, u32[]{:S(2)}) collective-permute-start(f32[128,512]{0,1:T(8,128)S(1)} %add.172), channel_id=1, source_target_pairs={{0,16},{1,17},{2,18},{3,19},{4,20},{5,21},{6,22},{7,23},{8,24},{9,... | collective-permute-start | bytes 786440 | tf_op jit(solution)/shard_map/ppermute | solution.py:10
  228.2 5.5 %collective-permute-start.14 = (f32[128,512]{0,1:T(8,128)S(1)}, f32[128,512]{0,1:T(8,128)S(1)}, u32[]{:S(2)}, u32[]{:S(2)}) collective-permute-start(f32[128,512]{0,1:T(8,128)S(1)} %add.173), channel_id=1, source_target_pairs={{0,32},{1,33},{2,34},{3,35},{4,36},{5,37},{6,38},{7,39},{8,40},{9,... | collective-permute-start | bytes 786440 | tf_op jit(solution)/shard_map/ppermute | solution.py:10
  271.0 6.4 %collective-permute-start.15 = (f32[128,384]{0,1:T(8,128)S(1)}, f32[128,384]{0,1:T(8,128)S(1)}, u32[]{:S(2)}, u32[]{:S(2)}) collective-permute-start(f32[128,384]{0,1:T(8,128)S(1)} %convolution_bitcast_fusion.3), channel_id=1, source_target_pairs={{0,1},{1,0},{2,3},{3,2},{4,5},{5,4},{6,7},{7,6},{8,9},{9,8},{10,11... | collective-permute-start | bytes 589832 | tf_op jit(solution)/shard_map/ppermute | solution.py:10
  277.4 6.2 %collective-permute-start.16 = (f32[128,384]{0,1:T(8,128)S(1)}, f32[128,384]{0,1:T(8,128)S(1)}, u32[]{:S(2)}, u32[]{:S(2)}) collective-permute-start(f32[128,384]{0,1:T(8,128)S(1)} %add.176), channel_id=1, source_target_pairs={{0,2},{1,3},{2,0},{3,1},{4,6},{5,7},{6,4},{7,5},{8,10},{9,11},{10,... | collective-permute-start | bytes 589832 | tf_op jit(solution)/shard_map/ppermute | solution.py:10
  283.6 6.8 %collective-permute-start.17 = (f32[128,384]{0,1:T(8,128)S(1)}, f32[128,384]{0,1:T(8,128)S(1)}, u32[]{:S(2)}, u32[]{:S(2)}) collective-permute-start(f32[128,384]{0,1:T(8,128)S(1)} %add.177), channel_id=1, source_target_pairs={{0,4},{1,5},{2,6},{3,7},{4,0},{5,1},{6,2},{7,3},{8,12},{9,13},{10,... | collective-permute-start | bytes 589832 | tf_op jit(solution)/shard_map/ppermute | solution.py:10
  290.4 4.6 collective-permute-start.18
  295.1 6.1 %collective-permute-start.19 = (f32[128,384]{0,1:T(8,128)S(1)}, f32[128,384]{0,1:T(8,128)S(1)}, u32[]{:S(2)}, u32[]{:S(2)}) collective-permute-start(f32[128,384]{0,1:T(8,128)S(1)} %add.179), channel_id=1, source_target_pairs={{0,16},{1,17},{2,18},{3,19},{4,20},{5,21},{6,22},{7,23},{8,24},{9,... | collective-permute-start | bytes 589832 | tf_op jit(solution)/shard_map/ppermute | solution.py:10
  301.2 4.6 collective-permute-start.20
  305.8 6.9 %collective-permute-start.21 = (f32[128,384]{0,1:T(8,128)S(1)}, f32[128,384]{0,1:T(8,128)S(1)}, u32[]{:S(2)}, u32[]{:S(2)}) collective-permute-start(f32[128,384]{0,1:T(8,128)S(1)} %add.181), channel_id=1, source_target_pairs={{0,64},{1,65},{2,66},{3,67},{4,68},{5,69},{6,70},{7,71},{8,72},{9,... | collective-permute-start | bytes 589832 | tf_op jit(solution)/shard_map/ppermute | solution.py:10
  340.2 36.2 %copy-start.5 = (f32[2048,256]{1,0:T(8,128)}, f32[2048,256]{1,0:T(8,128)S(1)}, u32[]{:S(2)}) copy-start(f32[2048,256]{1,0:T(8,128)S(1)} %convolution_subtract_fusion) | copy-start | bytes 6291460
  345.7 9.6 %collective-permute-start.22 = (f32[128,256]{0,1:T(8,128)S(1)}, f32[128,256]{0,1:T(8,128)S(1)}, u32[]{:S(2)}, u32[]{:S(2)}) collective-permute-start(f32[128,256]{0,1:T(8,128)S(1)} %convolution_bitcast_fusion.4), channel_id=1, source_target_pairs={{0,1},{1,0},{2,3},{3,2},{4,5},{5,4},{6,7},{7,6},{8,9},{9,8},{10,11... | collective-permute-start | bytes 393224 | tf_op jit(solution)/shard_map/ppermute | solution.py:10
  355.3 4.8 collective-permute-start.23
  360.1 5.4 %collective-permute-start.24 = (f32[128,256]{0,1:T(8,128)S(1)}, f32[128,256]{0,1:T(8,128)S(1)}, u32[]{:S(2)}, u32[]{:S(2)}) collective-permute-start(f32[128,256]{0,1:T(8,128)S(1)} %add.185), channel_id=1, source_target_pairs={{0,4},{1,5},{2,6},{3,7},{4,0},{5,1},{6,2},{7,3},{8,12},{9,13},{10,... | collective-permute-start | bytes 393224 | tf_op jit(solution)/shard_map/ppermute | solution.py:10
  365.5 3.9 collective-permute-start.25
  369.5 6.9 %collective-permute-start.26 = (f32[128,256]{0,1:T(8,128)S(1)}, f32[128,256]{0,1:T(8,128)S(1)}, u32[]{:S(2)}, u32[]{:S(2)}) collective-permute-start(f32[128,256]{0,1:T(8,128)S(1)} %add.187), channel_id=1, source_target_pairs={{0,16},{1,17},{2,18},{3,19},{4,20},{5,21},{6,22},{7,23},{8,24},{9,... | collective-permute-start | bytes 393224 | tf_op jit(solution)/shard_map/ppermute | solution.py:10
  376.4 3.9 collective-permute-start.27
  380.3 7.0 %collective-permute-start.28 = (f32[128,256]{0,1:T(8,128)S(1)}, f32[128,256]{0,1:T(8,128)S(1)}, u32[]{:S(2)}, u32[]{:S(2)}) collective-permute-start(f32[128,256]{0,1:T(8,128)S(1)} %add.189), channel_id=1, source_target_pairs={{0,64},{1,65},{2,66},{3,67},{4,68},{5,69},{6,70},{7,71},{8,72},{9,... | collective-permute-start | bytes 393224 | tf_op jit(solution)/shard_map/ppermute | solution.py:10
  387.4 9.5 %collective-permute-start.29 = (f32[128,256]{0,1:T(8,128)S(1)}, f32[128,256]{0,1:T(8,128)S(1)}, u32[]{:S(2)}, u32[]{:S(2)}) collective-permute-start(f32[128,256]{0,1:T(8,128)S(1)} %add.190), channel_id=1, source_target_pairs={{0,128},{1,129},{2,130},{3,131},{4,132},{5,133},{6,134},{7,135},{8... | collective-permute-start | bytes 393224 | tf_op jit(solution)/shard_map/ppermute | solution.py:10
  (5 other events, 41.2 us)
where the time goes:
time: 519 us; the launch traced here: 514 us
  waiting for transfers between devices  138 us (27%)
  other arithmetic  118 us (23%)
  blocking collectives  85.2 us (16%)
  matrix products  81.3 us (16%)
  starting transfers between devices  57.4 us (11%)
  local copies, waits for them, and re-layouts  27.3 us (5%)
  between operations  6.56 us (1%)
    ppermute x30, waiting for transfers between devices, swapped(): return lax.ppermute(value, axis, pairs)  138 us
    psum x1, blocking collectives, body(): total_log = lax.psum(log_share, 'leaf')  85.2 us
    another operation x15, other arithmetic, body(): factor = jnp.linalg.cholesky(capacity)  61.9 us
    ppermute x30, starting transfers between devices, swapped(): return lax.ppermute(value, axis, pairs)  57.4 us
    another operation x10, other arithmetic, cholesky_solve(): lax.linalg.triangular_solve(factor, middle, left_side=True, lower=True, t...  52.3 us
    dot_general x5, matrix products, body(): jnp.einsum('ir,ic->rc', basis, current, precision=lax.Precision.HIGHEST)  42.7 us
    dot_general x5, matrix products, body(): jnp.dot(current[:, :rank_size], weights, precision=lax.Precision.HIGHEST,...  26.7 us
    concatenate x2, local copies, waits for them, and re-layouts, body(): jnp.concatenate([node_bases.reshape(row_count, level_count * rank_size),...  17.1 us
  transfers between devices with their start and end apart: 30, of which 28 were waited for; matrix products, arithmetic and copies ran while one was open for 1% of the time, Pallas kernels for 0%

commit v1 on v0

v1 whole, which is shorter than its diff:
```python
import functools

import jax
import jax.numpy as jnp
from jax import lax
from jax.experimental import pallas as pl
from jax.experimental.pallas import tpu as pltpu
from jax.sharding import PartitionSpec as P

F32 = jnp.float32
BF16 = jnp.bfloat16
MESH = pl.DeviceIdType.MESH
R = 128
LEVELS = 5
OFFSET = (0, 6, 11, 15, 18, 20)
GROUP = 16
STEP = 16


def block(a, b):
    return OFFSET[a] + b - a


def halves(v):
    high = v.astype(BF16)
    return high, (v - high.astype(F32)).astype(BF16)


def dot3(a, b):
    ah, al = halves(a)
    bh, bl = halves(b)
    return jnp.dot(
        jnp.concatenate([ah, ah, al], axis=1),
        jnp.concatenate([bh, bl, bh], axis=0),
        preferred_element_type=F32,
    )


def tdot(a, b):
    return lax.dot_general(a, b, (((0,), (0,)), ((), ())), preferred_element_type=F32)


def tdot3(a, b):
    ah, al = halves(a)
    bh, bl = halves(b)
    return tdot(jnp.concatenate([ah, ah, al], axis=0), jnp.concatenate([bh, bl, bh], axis=0))


def dot_full(a, b):
    return jnp.dot(a, b, precision=lax.Precision.HIGHEST, preferred_element_type=F32)


def thirds(v):
    high = v.astype(BF16)
    rest = v - high.astype(F32)
    middle = rest.astype(BF16)
    low = (rest - middle.astype(F32)).astype(BF16)
    return high, middle, low


def sweep(a_ref):
    lane = lax.broadcasted_iota(jnp.int32, (STEP, R), 1)
    sub = lax.broadcasted_iota(jnp.int32, (STEP, R), 0)
    sub8 = lax.broadcasted_iota(jnp.int32, (8, R), 0)
    row_step = lax.broadcasted_iota(jnp.int32, (R, R), 0) // STEP
    column_step = lax.broadcasted_iota(jnp.int32, (R, R), 1) // STEP

    def pack(rows):
        groups = []
        for first in range(0, STEP, 8):
            packed = rows[first]
            for i in range(1, 8):
                packed = jnp.where(sub8 == i, rows[first + i], packed)
            groups.append(packed)
        return jnp.concatenate(groups, axis=0)

    def step(p, logs):
        base = pl.multiple_of(p * STEP, STEP)
        panel = a_ref[pl.ds(base, STEP), :]
        turned = pltpu.roll(panel, lax.rem(R - base, R), axis=1)
        q = jnp.where(lane // STEP == p, jnp.where(lane - base == sub, -1.0, 0.0), panel)
        rows = []
        for i in range(STEP):
            entries = [jnp.broadcast_to(turned[i : i + 1, j : j + 1], (8, R)) for j in range(i, STEP)]
            entries.append(jnp.broadcast_to(q[i : i + 1, :], (8, R)))
            rows.append(jnp.stack(entries))
        inverses = []
        for k in range(STEP):
            inverses.append(1.0 / rows[k][0])
            for i in range(k + 1, STEP):
                ratio = rows[k][i - k] * inverses[k]
                rows[i] = rows[i] - ratio[None] * rows[k][i - k :]
        v = pack([rows[i][STEP - i] for i in range(STEP)])
        w = v * pack(inverses)
        pivots = pack([rows[i][0] for i in range(STEP)])
        vh, vm, vl = thirds(v)
        wh, wm, wl = thirds(w)
        change = tdot(
            jnp.concatenate([vh, vh, vm, vh, vm, vl], axis=0),
            jnp.concatenate([wh, wm, wh, wl, wm, wh], axis=0),
        )
        a_ref[...] = jnp.where((row_step == p) | (column_step == p), 0.0, a_ref[...]) - change
        taken = jnp.log(pivots)
        return logs + taken[:8] + taken[8:]

    return lax.fori_loop(0, R // STEP, step, jnp.zeros((8, R), F32))


def kernel(
    d_hbm, u_hbm, b_hbm, o_hbm, log_ref,
    dv, uv, bv, xv, ov, g, r0, rc, h, r1,
    pc0, pc1, pc2, pc3, pc4, sx1, sx2, sx3, sx4, rx1, rx2, rx3, rx4,
    f0, f1, f2, f3, f4, t0, t1, t2, t3, gt, a_ref, y,
    load_sem, out_sem, rs_send, rs_recv, x_send, x_recv, ag_send, ag_recv,
):
    leaves = d_hbm.shape[0]
    size = d_hbm.shape[1]
    pc = (pc0, pc1, pc2, pc3, pc4)
    sx = (None, sx1, sx2, sx3, sx4)
    rx = (None, rx1, rx2, rx3, rx4)
    f = (f0, f1, f2, f3, f4)
    t = (t0, t1, t2, t3)

    me = lax.axis_index("leaf")
    z = me // 32
    x = (me // 8) % 4
    half = x // 2
    x_in = x + half * (3 - 2 * x)
    seat = x_in * 8 + me % 8
    chip = seat // 2
    core = seat % 2
    piece = pl.multiple_of(seat * 8, 8)

    def device(other):
        xo = other // 8
        return z * 32 + (xo + half * (3 - 2 * xo)) * 8 + other % 8

    partner = (
        None,
        me + 8 * (3 - 2 * x),
        me + 32 * (1 - 2 * (z % 2)),
        me + 32 * (3 - 2 * (z % 4)),
        me + 32 * (7 - 2 * z),
    )

    barrier = pltpu.get_barrier_semaphore()

    def greet(r, carry):
        pl.semaphore_signal(barrier, inc=1, device_id=(device((seat + r) % GROUP),), device_id_type=MESH)
        return carry

    lax.fori_loop(1, GROUP, greet, 0)
    for e in range(1, LEVELS):
        pl.semaphore_signal(barrier, inc=1, device_id=(partner[e],), device_id_type=MESH)

    def rows_of(leaf):
        return pl.ds(pl.multiple_of(leaf * size, size), size)

    def load_d(leaf):
        return pltpu.make_async_copy(d_hbm.at[leaf], dv.at[leaf], load_sem.at[0, leaf])

    def load_u0(leaf):
        return pltpu.make_async_copy(
            u_hbm.at[pl.ds(0, 1), rows_of(leaf), :], uv.at[pl.ds(0, 1), rows_of(leaf), :], load_sem.at[1, leaf]
        )

    def load_u(leaf):
        return pltpu.make_async_copy(
            u_hbm.at[pl.ds(1, LEVELS - 1), rows_of(leaf), :],
            uv.at[pl.ds(1, LEVELS - 1), rows_of(leaf), :],
            load_sem.at[2, leaf],
        )

    def load_b(leaf):
        return pltpu.make_async_copy(b_hbm.at[rows_of(leaf), :], bv.at[rows_of(leaf), :], load_sem.at[3, leaf])

    for leaf in range(leaves):
        load_d(leaf).start()
        load_u0(leaf).start()
    for leaf in range(leaves):
        load_u(leaf).start()
        load_b(leaf).start()

    def remote(source, target, send, recv, who):
        return pltpu.make_async_remote_copy(
            src_ref=source, dst_ref=target, send_sem=send, recv_sem=recv,
            device_id=(who,), device_id_type=MESH,
        )

    def first_leaf(leaf, total):
        load_d(leaf).wait()
        load_u0(leaf).wait()
        u0 = uv[0, rows_of(leaf), :]
        x0 = dot3(dv[leaf], u0)
        xv[0, rows_of(leaf), :] = x0
        return total + tdot3(u0, x0)

    total = lax.fori_loop(0, leaves, first_leaf, jnp.zeros((R, R), F32))
    g[0] = total.reshape(8, 2, 8, R)

    pl.semaphore_wait(barrier, GROUP - 1 + LEVELS - 1)

    def send_first(r, carry):
        other = (seat + r) % GROUP
        remote(
            g.at[pl.ds(0, 1), other // 2, other % 2], r0.at[r - 1],
            rs_send.at[0], rs_recv.at[0], device(other),
        ).start()
        return carry

    lax.fori_loop(1, GROUP, send_first, 0)

    g[pl.ds(1, 19)] = jnp.zeros((19, 8, 2, 8, R), F32)

    def add_block(a, b, value):
        g[block(a, b)] = g[block(a, b)] + value.reshape(8, 2, 8, R)

    def next_leaf(leaf, carry):
        load_u(leaf).wait()
        load_b(leaf).wait()
        u = [uv[j, rows_of(leaf), :] for j in range(LEVELS)]
        values = jnp.concatenate(u[1:] + [bv[rows_of(leaf), :]], axis=1)
        got = dot3(dv[leaf], values)
        for k in range(1, LEVELS + 1):
            xv[k, rows_of(leaf), :] = got[:, R * (k - 1) : R * k]
        for columns, top in (((1, 2), 2), ((3, 4), 4), ((5,), 4)):
            part = got[:, R * (columns[0] - 1) : R * columns[-1]]
            products = tdot3(jnp.concatenate(u[: top + 1], axis=1), part)
            for k in columns:
                for j in range(min(k, LEVELS - 1) + 1):
                    at = R * (k - columns[0])
                    add_block(j, k, products[R * j : R * (j + 1), at : at + R])
        return carry

    def sum_first():
        remote(r0, r0, rs_send.at[0], rs_recv.at[0], me).wait_recv()
        kept = g[0, chip, core]
        for r in range(GROUP - 1):
            kept = kept + r0[r, 0]
        pc0[0] = kept

    def gather(level, first, count, slot):
        for b in range(first, first + count):
            f[level][b, pl.ds(piece, 8), :] = pc[level][b]

        def one(r, carry):
            other = (seat + r) % GROUP
            remote(
                pc[level].at[pl.ds(first, count)],
                f[level].at[pl.ds(first, count), pl.ds(piece, 8), :],
                ag_send.at[level, slot], ag_recv.at[level, slot], device(other),
            ).start()
            return carry

        lax.fori_loop(1, GROUP, one, 0)

    def gathered(level, first, count, slot):
        ref = f[level].at[pl.ds(first, count), pl.ds(0, 120), :]
        return remote(ref, ref, ag_send.at[level, slot], ag_recv.at[level, slot], me)

    lax.fori_loop(0, leaves // 2, next_leaf, 0)
    sum_first()
    gather(0, 0, 1, 0)
    lax.fori_loop(leaves // 2, leaves, next_leaf, 0)

    mate = me + 1 - 2 * core
    to_mate = remote(
        g.at[pl.ds(1, 19), pl.ds(0, 8), 1 - core], rc, rs_send.at[1], rs_recv.at[1], mate
    )
    to_mate.start()
    to_mate.wait_recv()

    def add_core(i, carry):
        h[i] = g[i + 1, :, core] + rc[i]
        return carry

    lax.fori_loop(0, 19, add_core, 0)

    def send_rest(r, carry):
        other = (chip + r) % 8
        remote(
            h.at[pl.ds(0, 19), other], r1.at[r - 1],
            rs_send.at[2], rs_recv.at[2], device(other * 2 + core),
        ).start()
        return carry

    lax.fori_loop(1, 8, send_rest, 0)

    eye = (
        lax.broadcasted_iota(jnp.int32, (R, R), 0) == lax.broadcasted_iota(jnp.int32, (R, R), 1)
    ).astype(F32)
    logs = jnp.zeros((8, R), F32)

    for level in range(LEVELS):
        gathered(level, 0, 1, 0).wait_recv()
        a_ref[...] = f[level][0] + eye
        logs = logs + sweep(a_ref)
        inverse = -a_ref[...]
        count = LEVELS - level
        if level == 0:
            remote(r1, r1, rs_send.at[2], rs_recv.at[2], me).wait_recv()
            kept = h[:, chip]
            for r in range(7):
                kept = kept + r1[r]
            pc0[pl.ds(1, 19)] = kept
            gather(0, 1, count, 1)
        gathered(level, 1, count, 1).wait_recv()
        if level == LEVELS - 1:
            y[pl.ds(R * level, R), :] = dot_full(inverse, f[level][1])
            break
        row = jnp.concatenate([f[level][i] for i in range(1, count + 1)], axis=1)
        ratio = dot_full(inverse, row)
        t[level][...] = ratio
        for a in range(count - 1):
            gt[a] = f[level][a + 1].T
        left = jnp.concatenate([gt[a, pl.ds(piece, 8), :] for a in range(count - 1)], axis=0)
        down = dot_full(left, ratio)
        e = level + 1
        skip = OFFSET[e] - OFFSET[level]
        for a in range(e, LEVELS):
            for b in range(a, LEVELS + 1):
                i = block(a, b) - OFFSET[e]
                sx[e][i] = pc[level][i + skip] - down[8 * (a - e) : 8 * (a - e) + 8, R * (b - e) : R * (b - e) + R]
        total_blocks = 20 - OFFSET[e]
        sx[e][total_blocks] = logs
        swap = [
            remote(
                sx[e].at[pl.ds(first, n)], rx[e].at[pl.ds(first, n)],
                x_send.at[e, slot], x_recv.at[e, slot], partner[e],
            )
            for slot, first, n in ((0, 0, 1), (1, 1, total_blocks))
        ]
        swap[0].start()
        swap[1].start()
        swap[0].wait_recv()
        pc[e][0] = sx[e][0] + rx[e][0]
        gather(e, 0, 1, 0)
        swap[1].wait_recv()
        pc[e][pl.ds(1, total_blocks)] = sx[e][pl.ds(1, total_blocks)] + rx[e][pl.ds(1, total_blocks)]
        gather(e, 1, count - 1, 1)
        logs = pc[e][total_blocks]

    for level in range(LEVELS - 2, -1, -1):
        known = R * (LEVELS - 1 - level)
        y[pl.ds(R * level, R), :] = t[level][:, known:] - dot_full(
            t[level][:, :known], y[pl.ds(R * (level + 1), known), :]
        )
    y_high, y_low = halves(y[...])
    y_stack = jnp.concatenate([y_high, y_low, y_high], axis=0)

    def store(leaf):
        return pltpu.make_async_copy(ov.at[rows_of(leaf), :], o_hbm.at[rows_of(leaf), :], out_sem.at[leaf])

    def last_leaf(leaf, carry):
        have = jnp.concatenate([xv[k, rows_of(leaf), :] for k in range(LEVELS)], axis=1)
        high, low = halves(have)
        change = jnp.dot(jnp.concatenate([high, high, low], axis=1), y_stack, preferred_element_type=F32)
        ov[rows_of(leaf), :] = xv[LEVELS, rows_of(leaf), :] - change
        store(leaf).start()
        return carry

    lax.fori_loop(0, leaves, last_leaf, 0)
    log_ref[0, 0] = jnp.sum(logs) / (R * R * (2**LEVELS - 1))

    remote(r0, r0, rs_send.at[0], rs_recv.at[0], me).wait_send()
    to_mate.wait_send()
    remote(r1, r1, rs_send.at[2], rs_recv.at[2], me).wait_send()
    for level in range(LEVELS):
        gathered(level, 0, 1, 0).wait_send()
        gathered(level, 1, LEVELS - level, 1).wait_send()
    for e in range(1, LEVELS):
        n = 20 - OFFSET[e]
        remote(sx[e].at[pl.ds(0, 1)], rx[e].at[pl.ds(0, 1)], x_send.at[e, 0], x_recv.at[e, 0], me).wait_send()
        remote(sx[e].at[pl.ds(1, n)], rx[e].at[pl.ds(1, n)], x_send.at[e, 1], x_recv.at[e, 1], me).wait_send()

    def finish(leaf, carry):
        store(leaf).wait()
        return carry

    lax.fori_loop(0, leaves, finish, 0)


def body(leaf_inverse, node_bases, right_sides):
    leaves, size = leaf_inverse.shape[:2]
    rows = right_sides.shape[0]
    bases = jnp.transpose(node_bases, (1, 0, 2))
    vm = pltpu.VMEM
    sizes = [20 - OFFSET[e] + 1 for e in range(LEVELS)]
    any_spec = pl.BlockSpec(memory_space=pl.ANY)
    scratch = [
        vm((leaves, size, size), F32), vm((LEVELS, rows, R), F32), vm((rows, R), F32),
        vm((LEVELS + 1, rows, R), F32), vm((rows, R), F32),
        vm((20, 8, 2, 8, R), F32), vm((GROUP - 1, 1, 8, R), F32), vm((19, 8, 8, R), F32),
        vm((19, 8, 8, R), F32), vm((7, 19, 8, R), F32),
    ]
    scratch += [vm((n, 8, R), F32) for n in [20] + sizes[1:]]
    scratch += [vm((n, 8, R), F32) for n in sizes[1:]]
    scratch += [vm((n, 8, R), F32) for n in sizes[1:]]
    scratch += [vm((LEVELS + 1 - level, R, R), F32) for level in range(LEVELS)]
    scratch += [vm((R, R * (LEVELS - level)), F32) for level in range(LEVELS - 1)]
    scratch += [vm((LEVELS - 1, R, R), F32), vm((R, R), F32), vm((LEVELS * R, R), F32)]
    dma = pltpu.SemaphoreType.DMA
    scratch += [
        dma((4, leaves)), dma((leaves,)), dma((3,)), dma((3,)),
        dma((LEVELS, 2)), dma((LEVELS, 2)), dma((LEVELS, 2)), dma((LEVELS, 2)),
    ]
    solution, log_total = pl.pallas_call(
        kernel,
        out_shape=(
            jax.ShapeDtypeStruct((rows, R), F32),
            jax.ShapeDtypeStruct((1, 1), F32),
        ),
        in_specs=[any_spec] * 3,
        out_specs=(any_spec, pl.BlockSpec(memory_space=pltpu.SMEM)),
        scratch_shapes=scratch,
        compiler_params=pltpu.CompilerParams(
            collective_id=0, has_side_effects=True, vmem_limit_bytes=60 * 2**20
        ),
    )(leaf_inverse, bases, right_sides)
    return solution, log_total.reshape(())


def solution(mesh):
    return jax.shard_map(
        body,
        mesh=mesh,
        in_specs=(P("leaf", None, None), P("leaf", None, None), P("leaf", None)),
        out_specs=(P("leaf", None), P()),
        check_vma=False,
    )
```

time: 519 us -> 106 us (0.20)
  waiting for transfers between devices: 138 us -> 0 us
  other arithmetic: 118 us -> 0 us
  Pallas kernels: 0 us -> 101 us
  blocking collectives: 85.2 us -> 0 us
  matrix products: 81.3 us -> 0 us
  starting transfers between devices: 57.4 us -> 0 us
  local copies, waits for them, and re-layouts: 27.3 us -> 2.26 us
    ppermute x30 -> x0, waiting for transfers between devices: 138 us -> none  [swapped(): return lax.ppermute(value, axis, pairs)]
    another operation x25 -> x0, other arithmetic: 114 us -> none  [the longest x15 61.9 us: body(): factor = jnp.linalg.cholesky(capacity)]
    pallas_call x0 -> x1, Pallas kernels: none -> 101 us  [body(): pl.pallas_call(kernel, out_shape=(jax.ShapeDtypeStruct((rows, R), F32), j...]
    psum x1 -> x0, blocking collectives: 85.2 us -> none  [body(): total_log = lax.psum(log_share, 'leaf')]
    dot_general x11 -> x0, matrix products: 77.8 us -> none  [the longest x5 42.7 us: body(): jnp.einsum('ir,ic->rc', basis, current, precision=lax.Precision.HIGHEST)]
    ppermute x30 -> x0, starting transfers between devices: 57.4 us -> none  [swapped(): return lax.ppermute(value, axis, pairs)]
    concatenate x2 -> x0, local copies, waits for them, and re-layouts: 17.1 us -> none  [body(): jnp.concatenate([node_bases.reshape(row_count, level_count * rank_size),...]
    gather x5 -> x0, local copies, waits for them, and re-layouts: 6.22 us -> none  [body(): jnp.diagonal(factor)]
  transfers between devices with their start and end apart: 30 -> 0, of which waited for: 28 -> 0; matrix products, arithmetic and copies ran while one was open for 1% -> 0% of each run, Pallas kernels for 0% -> 0%
where the time goes in v1:
time: 106 us
  Pallas kernels  101 us (95%)
  between operations  2.33 us (2%)
  local copies, waits for them, and re-layouts  2.26 us (2%)
    pallas_call x1, Pallas kernels, body(): pl.pallas_call(kernel, out_shape=(jax.ShapeDtypeStruct((rows, R), F32), j...  101 us
    unnamed x1, local copies, waits for them, and re-layouts  2.26 us

profile of v1, /device:TPU:1, one launch (start us, length us, event | category | flops | bytes accessed | tf_op | source)
XLA Modules:
  0.0 105.7 jit_solution(17841913725108493888)
XLA Ops:
  0.6 101.1 %shard_map.50 = (f32[2048,128]{1,0:T(8,128)}, f32[1,1]{1,0:T(1,128)}) custom-call(f32[8,256,256]{2,1,0:T(8,128)} %d_hbm.1, f32[5,2048,128]{2,1,0:T(8,128)} %bitcast.2, f32[2048,128]{1,0:T(8,128)} %b_hbm.1), custom_call_target="tpu_custom_call" | custom-call | tf_op jit(solution)/shard_map/pallas_call | solution.py:407
  101.8 2.3 %copy.7 = f32[2048,128]{1,0:T(8,128)} copy(f32[2048,128]{1,0:T(8,128)} %get-tuple-element.8) | data formatting | bytes 2097152

commit v2 on v0

v2 whole, which is shorter than its diff:
```python
import functools

import jax
import jax.numpy as jnp
from jax import lax
from jax.experimental import pallas as pl
from jax.experimental.pallas import tpu as pltpu
from jax.sharding import PartitionSpec as P

F32 = jnp.float32
BF16 = jnp.bfloat16
MESH = pl.DeviceIdType.MESH
R = 128
LEVELS = 5
LEVEL_COLUMNS = LEVELS + 1
GROUP = 16
STEP = 16

ORDER = (
    (0, 0), (0, 1), (1, 1),
    (0, 2), (0, 3), (1, 2), (2, 2), (1, 3), (2, 3), (3, 3),
    (0, 4), (0, 5), (1, 4), (1, 5), (2, 4), (2, 5), (3, 4), (4, 4), (3, 5), (4, 5),
)
COUNT = len(ORDER)
A, B, END = 3, 10, COUNT
GATHERS = {
    "d0": (0, 1), "c0": (1, 3), "a0": (3, 5), "b0": (10, 12), "a1": (5, 8), "b1": (12, 14),
    "a2": (8, 10), "b2": (14, 16), "b3": (16, 19), "b4": (19, 20),
}
SWAPS = {"a1": (5, 10), "b1": (12, 20), "a2": (8, 10), "b2": (14, 20), "b3": (16, 20), "b4": (19, 20)}
GATHER_SLOT = {name: i for i, name in enumerate(GATHERS)}
SWAP_SLOT = {name: i for i, name in enumerate(SWAPS)}


def block(a, b):
    return ORDER.index((a, b))


def halves(v):
    high = v.astype(BF16)
    return high, (v - high.astype(F32)).astype(BF16)


def dot3(a, b):
    ah, al = halves(a)
    bh, bl = halves(b)
    return jnp.dot(
        jnp.concatenate([ah, ah, al], axis=1),
        jnp.concatenate([bh, bl, bh], axis=0),
        preferred_element_type=F32,
    )


def tdot(a, b):
    return lax.dot_general(a, b, (((0,), (0,)), ((), ())), preferred_element_type=F32)


def tdot3(a, b):
    ah, al = halves(a)
    bh, bl = halves(b)
    return tdot(jnp.concatenate([ah, ah, al], axis=0), jnp.concatenate([bh, bl, bh], axis=0))


def dot_full(a, b):
    return jnp.dot(a, b, precision=lax.Precision.HIGHEST, preferred_element_type=F32)


def thirds(v):
    high = v.astype(BF16)
    rest = v - high.astype(F32)
    middle = rest.astype(BF16)
    low = (rest - middle.astype(F32)).astype(BF16)
    return high, middle, low


def sweep(a_ref, column_ref, q_ref, log_ref, tasks):
    lane = lax.broadcasted_iota(jnp.int32, (STEP, R), 1)
    sub = lax.broadcasted_iota(jnp.int32, (STEP, R), 0)
    sub8 = lax.broadcasted_iota(jnp.int32, (8, R), 0)
    row_step = lax.broadcasted_iota(jnp.int32, (R, R), 0) // STEP
    column_step = lax.broadcasted_iota(jnp.int32, (R, R), 1) // STEP

    def pack(rows):
        groups = []
        for first in range(0, STEP, 8):
            packed = rows[first]
            for i in range(1, 8):
                packed = jnp.where(sub8 == i, rows[first + i], packed)
            groups.append(packed)
        return jnp.concatenate(groups, axis=0)

    def step(p, carry):
        for at, task in tasks.items():
            pl.when(p == at)(task)
        base = pl.multiple_of(p * STEP, STEP)
        panel = a_ref[pl.ds(base, STEP), :]
        turned = pltpu.roll(panel, lax.rem(R - base, R), axis=1)
        for j in range(STEP):
            high = (j // 8 + 1) * 8
            column_ref[pl.ds(j * STEP, high), :] = jnp.broadcast_to(turned[:high, j : j + 1], (high, R))
        q_ref[pl.ds(0, STEP), :] = jnp.where(
            lane // STEP == p, jnp.where(lane - base == sub, -1.0, 0.0), panel
        )
        rows, ratios, inverses = [], [], []
        for i in range(STEP):
            row = [column_ref[pl.ds(j * STEP + i, 8, stride=0), :] for j in range(i, STEP)]
            row.append(q_ref[pl.ds(i, 8, stride=0), :])
            row = jnp.stack(row)
            for m in range(i):
                row = row - ratios[m][i - m][None] * rows[m][i - m :]
            inverse = 1.0 / row[0]
            rows.append(row)
            inverses.append(inverse)
            ratios.append(row[: STEP - i] * inverse[None])
        v = pack([rows[i][STEP - i] for i in range(STEP)])
        w = v * pack(inverses)
        pivots = pack([rows[i][0] for i in range(STEP)])
        vh, vm, vl = thirds(v)
        wh, wm, wl = thirds(w)
        change = tdot(
            jnp.concatenate([vh, vh, vm, vh, vm, vl], axis=0),
            jnp.concatenate([wh, wm, wh, wl, wm, wh], axis=0),
        )
        a_ref[...] = jnp.where((row_step == p) | (column_step == p), 0.0, a_ref[...]) - change
        taken = jnp.log(pivots)
        log_ref[...] = log_ref[...] + taken[:8] + taken[8:]
        return carry

    lax.fori_loop(0, R // STEP, step, 0)


def kernel(
    d_hbm, u_hbm, b_hbm, o_hbm, total_ref,
    dv, uv, bv, xv, ov, ab, g, rd, rs, ra, rb, ha, hb, qa, qb,
    pc, sx, rx, dx, dr, f, iv, tv, gt, zv, a_ref, column_ref, q_ref, log_ref,
    load_sem, out_sem, rs_send, rs_recv, d_send, d_recv, x_send, x_recv, g_send, g_recv,
):
    leaves = d_hbm.shape[0]
    size = d_hbm.shape[1]

    me = lax.axis_index("leaf")
    z = me // 32
    x = (me // 8) % 4
    half = x // 2
    x_in = x + half * (3 - 2 * x)
    seat = x_in * 8 + me % 8
    chip = seat // 2
    core = seat % 2
    piece = pl.multiple_of(seat * 8, 8)

    def device(other):
        xo = other // 8
        return z * 32 + (xo + half * (3 - 2 * xo)) * 8 + other % 8

    mate = me + 1 - 2 * core
    partner = (
        None,
        me + 8 * (3 - 2 * x),
        me + 32 * (1 - 2 * (z % 2)),
        me + 32 * (3 - 2 * (z % 4)),
        me + 32 * (7 - 2 * z),
    )

    barrier = pltpu.get_barrier_semaphore()

    def greet(r, carry):
        pl.semaphore_signal(barrier, inc=1, device_id=(device((seat + r) % GROUP),), device_id_type=MESH)
        return carry

    lax.fori_loop(1, GROUP, greet, 0)
    for e in range(1, LEVELS):
        pl.semaphore_signal(barrier, inc=1, device_id=(partner[e],), device_id_type=MESH)

    def rows_of(leaf):
        return pl.ds(pl.multiple_of(leaf * size, size), size)

    def load_d(leaf):
        return pltpu.make_async_copy(d_hbm.at[leaf], dv.at[leaf], load_sem.at[0, leaf])

    def load_u(leaf, first, count, slot):
        at = (pl.ds(first, count), rows_of(leaf), slice(None))
        return pltpu.make_async_copy(u_hbm.at[at], uv.at[at], load_sem.at[slot, leaf])

    def load_b(leaf):
        return pltpu.make_async_copy(b_hbm.at[rows_of(leaf), :], bv.at[rows_of(leaf), :], load_sem.at[4, leaf])

    for leaf in range(leaves):
        load_d(leaf).start()
        load_u(leaf, 0, 2, 1).start()
    for leaf in range(leaves):
        load_u(leaf, 2, 2, 2).start()
    for leaf in range(leaves):
        load_u(leaf, 4, 1, 3).start()
        load_b(leaf).start()

    def remote(source, target, send, recv, who):
        return pltpu.make_async_remote_copy(
            src_ref=source, dst_ref=target, send_sem=send, recv_sem=recv,
            device_id=(who,), device_id_type=MESH,
        )

    g[...] = jnp.zeros((COUNT, 8, 2, 8, R), F32)

    def columns_of(leaf, columns):
        top = min(columns[-1], LEVELS - 1)
        u = [uv[j, rows_of(leaf), :] for j in range(top + 1)]
        have = [u[k] if k < LEVELS else bv[rows_of(leaf), :] for k in columns]
        got = dot3(dv[leaf], jnp.concatenate(have, axis=1))
        products = tdot3(jnp.concatenate(u, axis=1), got)
        for i, k in enumerate(columns):
            xv[k, rows_of(leaf), :] = got[:, R * i : R * (i + 1)]
            for j in range(min(k, LEVELS - 1) + 1):
                at = block(j, k)
                g[at] = g[at] + products[R * j : R * (j + 1), R * i : R * (i + 1)].reshape(8, 2, 8, R)

    def leaf_first(leaf, carry):
        load_d(leaf).wait()
        load_u(leaf, 0, 2, 1).wait()
        columns_of(leaf, (0, 1))
        return carry

    def leaf_second(leaf, carry):
        load_u(leaf, 2, 2, 2).wait()
        columns_of(leaf, (2, 3))
        return carry

    def leaf_third(leaf, carry):
        load_u(leaf, 4, 1, 3).wait()
        load_b(leaf).wait()
        columns_of(leaf, (4, 5))
        return carry

    def scatter(first, count, target, slot):
        def one(r, carry):
            other = (seat + r) % GROUP
            remote(
                g.at[pl.ds(first, count), other // 2, other % 2], target.at[r - 1],
                rs_send.at[slot], rs_recv.at[slot], device(other),
            ).start()
            return carry

        lax.fori_loop(1, GROUP, one, 0)

    def scattered(first, count, target, slot):
        remote(target, target, rs_send.at[slot], rs_recv.at[slot], me).wait_recv()
        kept = g[pl.ds(first, count), chip, core]
        for r in range(GROUP - 1):
            kept = kept + target[r]
        pc[pl.ds(first, count)] = kept

    def to_mate(first, count, target, slot):
        return remote(
            g.at[pl.ds(first, count), pl.ds(0, 8), 1 - core], target, rs_send.at[slot], rs_recv.at[slot], mate
        )

    def scatter_chips(first, count, from_mate, summed, target, slot):
        to_mate(first, count, from_mate, slot - 1).wait_recv()

        def add(i, carry):
            summed[i] = g[i + first, :, core] + from_mate[i]
            return carry

        lax.fori_loop(0, count, add, 0)

        def one(r, carry):
            other = (chip + r) % 8
            remote(
                summed.at[pl.ds(0, count), other], target.at[r - 1],
                rs_send.at[slot], rs_recv.at[slot], device(other * 2 + core),
            ).start()
            return carry

        lax.fori_loop(1, 8, one, 0)

    def scattered_chips(first, count, summed, target, slot):
        remote(target, target, rs_send.at[slot], rs_recv.at[slot], me).wait_recv()
        kept = summed[:, chip]
        for r in range(7):
            kept = kept + target[r]
        pc[pl.ds(first, count)] = kept

    def gather(name):
        first, last = GATHERS[name]
        slot = GATHER_SLOT[name]
        f[pl.ds(first, last - first), pl.ds(piece, 8), :] = pc[pl.ds(first, last - first)]

        def one(r, carry):
            other = (seat + r) % GROUP
            remote(
                pc.at[pl.ds(first, last - first)],
                f.at[pl.ds(first, last - first), pl.ds(piece, 8), :],
                g_send.at[slot], g_recv.at[slot], device(other),
            ).start()
            return carry

        lax.fori_loop(1, GROUP, one, 0)

    def gathered(name):
        first, last = GATHERS[name]
        slot = GATHER_SLOT[name]
        ref = f.at[pl.ds(first, last - first), pl.ds(0, 120), :]
        return remote(ref, ref, g_send.at[slot], g_recv.at[slot], me)

    def diagonal(e):
        return remote(dx.at[e - 1], dr.at[e - 1], d_send.at[e - 1], d_recv.at[e - 1], partner[e])

    def swap(name):
        first, last = SWAPS[name]
        e = int(name[1])
        slot = SWAP_SLOT[name]
        at = pl.ds(first, last - first)
        return remote(sx.at[e - 1, at], rx.at[e - 1, at], x_send.at[slot], x_recv.at[slot], partner[e])

    def turn(level, k):
        gt[level, k] = f[block(level, k)].T

    def critical(level):
        e = level + 1
        ratio = dot_full(iv[level], f[block(level, e)])
        tv[level, e] = ratio
        dx[e - 1, pl.ds(0, R), :] = f[block(e, e)] - dot_full(gt[level, e], ratio)
        dx[e - 1, pl.ds(R, 8), :] = log_ref[...]
        diagonal(e).start()

    def lower(level, columns, name):
        e = level + 1
        first, last = SWAPS[name]
        fresh = [k for k in columns if k != e]
        ratio = dot_full(iv[level], jnp.concatenate([f[block(level, k)] for k in fresh], axis=1))
        for i, k in enumerate(fresh):
            tv[level, k] = ratio[:, R * i : R * (i + 1)]
            if k < LEVELS:
                turn(level, k)
        ends = [r for r in range(e, LEVELS) if r <= columns[-1]]
        left = jnp.concatenate([gt[level, r, pl.ds(piece, 8), :] for r in ends], axis=0)
        down = dot_full(left, ratio)
        for at in range(first, last):
            r, k = ORDER[at]
            i = fresh.index(k)
            sx[e - 1, at] = pc[at] - down[8 * (r - e) : 8 * (r - e) + 8, R * i : R * (i + 1)]
        swap(name).start()

    def merge(name):
        first, last = SWAPS[name]
        e = int(name[1])
        swap(name).wait_recv()
        at = pl.ds(first, last - first)
        pc[at] = sx[e - 1, at] + rx[e - 1, at]
        gather(name)

    def enter(e):
        diagonal(e).wait_recv()
        a_ref[...] = dx[e - 1, pl.ds(0, R), :] + dr[e - 1, pl.ds(0, R), :] + eye
        log_ref[...] = dx[e - 1, pl.ds(R, 8), :] + dr[e - 1, pl.ds(R, 8), :]

    def invert(level, tasks):
        sweep(a_ref, column_ref, q_ref, log_ref, tasks)
        iv[level] = -a_ref[...]

    eye = (
        lax.broadcasted_iota(jnp.int32, (R, R), 0) == lax.broadcasted_iota(jnp.int32, (R, R), 1)
    ).astype(F32)

    lax.fori_loop(0, leaves, leaf_first, 0)
    pl.semaphore_wait(barrier, GROUP - 1 + LEVELS - 1)
    scatter(0, 1, rd, 0)
    scatter(1, 2, rs, 1)
    lax.fori_loop(0, leaves, leaf_second, 0)
    scattered(0, 1, rd, 0)
    gather("d0")
    to_mate(A, B - A, ra, 2).start()
    lax.fori_loop(0, leaves, leaf_third, 0)
    to_mate(B, END - B, rb, 4).start()
    scattered(1, 2, rs, 1)
    gather("c0")
    scatter_chips(A, B - A, ra, ha, qa, 3)
    gathered("d0").wait_recv()
    a_ref[...] = f[0] + eye
    log_ref[...] = jnp.zeros((8, R), F32)

    def task_0():
        scatter_chips(B, END - B, rb, hb, qb, 5)

    invert(0, {4: task_0})
    gathered("c0").wait_recv()
    turn(0, 1)
    critical(0)
    scattered_chips(A, B - A, ha, qa, 3)
    gather("a0")
    scattered_chips(B, END - B, hb, qb, 5)
    gather("b0")
    gathered("a0").wait_recv()
    lower(0, (2, 3), "a1")

    enter(1)

    def task_1a():
        merge("a1")

    def task_1b():
        gathered("b0").wait_recv()
        lower(0, (4, 5), "b1")

    invert(1, {3: task_1a, 5: task_1b})
    gathered("a1").wait_recv()
    turn(1, 2)
    critical(1)
    lower(1, (2, 3), "a2")
    merge("b1")

    enter(2)
    merge("a2")

    def task_2a():
        gathered("b1").wait_recv()
        lower(1, (4, 5), "b2")

    def task_2b():
        merge("b2")

    invert(2, {2: task_2a, 6: task_2b})
    gathered("a2").wait_recv()
    turn(2, 3)
    critical(2)

    gathered("b2").wait_recv()
    lower(2, (4, 5), "b3")
    enter(3)

    def task_3():
        merge("b3")

    invert(3, {3: task_3})
    gathered("b3").wait_recv()
    turn(3, 4)
    critical(3)
    lower(3, (4, 5), "b4")

    for level in range(LEVELS - 2, -1, -1):
        pair = jnp.concatenate([tv[level, 4], tv[level, 5]], axis=1)
        if level < LEVELS - 2:
            between = jnp.concatenate([tv[level, k] for k in range(level + 1, LEVELS - 1)], axis=1)
            pair = pair - dot_full(between, zv[pl.ds(R * (level + 1), R * (LEVELS - 2 - level)), :])
        zv[pl.ds(R * level, R), :] = pair
    z_high, z_low = halves(zv[...])
    z_stack = jnp.concatenate([z_high, z_low, z_high], axis=0)

    def update(leaf, carry):
        high, low = halves(jnp.concatenate([xv[k, rows_of(leaf), :] for k in range(LEVELS - 1)], axis=1))
        change = jnp.dot(jnp.concatenate([high, high, low], axis=1), z_stack, preferred_element_type=F32)
        ab[rows_of(leaf), :] = jnp.concatenate([xv[k, rows_of(leaf), :] for k in (4, 5)], axis=1) - change
        return carry

    lax.fori_loop(0, leaves, update, 0)

    merge("b4")
    enter(4)
    invert(4, {})
    gathered("b4").wait_recv()
    weights = dot_full(iv[4], f[block(4, 5)])
    w_high, w_low = halves(weights)
    w_stack = jnp.concatenate([w_high, w_low, w_high], axis=0)

    def store(leaf):
        return pltpu.make_async_copy(ov.at[rows_of(leaf), :], o_hbm.at[rows_of(leaf), :], out_sem.at[leaf])

    def last(leaf, carry):
        high, low = halves(ab[rows_of(leaf), pl.ds(0, R)])
        change = jnp.dot(jnp.concatenate([high, high, low], axis=1), w_stack, preferred_element_type=F32)
        ov[rows_of(leaf), :] = ab[rows_of(leaf), pl.ds(R, R)] - change
        store(leaf).start()
        return carry

    lax.fori_loop(0, leaves, last, 0)
    total_ref[0, 0] = jnp.sum(log_ref[...]) / (R * R * (2**LEVELS - 1))

    for target, slot in ((rd, 0), (rs, 1), (qa, 3), (qb, 5)):
        remote(target, target, rs_send.at[slot], rs_recv.at[slot], me).wait_send()
    to_mate(A, B - A, ra, 2).wait_send()
    to_mate(B, END - B, rb, 4).wait_send()
    for name in GATHERS:
        gathered(name).wait_send()
    for name in SWAPS:
        swap(name).wait_send()
    for e in range(1, LEVELS):
        diagonal(e).wait_send()

    def finish(leaf, carry):
        store(leaf).wait()
        return carry

    lax.fori_loop(0, leaves, finish, 0)


def body(leaf_inverse, node_bases, right_sides):
    leaves, size = leaf_inverse.shape[:2]
    rows = right_sides.shape[0]
    bases = jnp.transpose(node_bases, (1, 0, 2))
    any_spec = pl.BlockSpec(memory_space=pl.ANY)
    na, nb = B - A, END - B
    shapes = [
        (leaves, size, size), (LEVELS, rows, R), (rows, R), (LEVEL_COLUMNS, rows, R), (rows, R), (rows, 2 * R),
        (COUNT, 8, 2, 8, R), (GROUP - 1, 1, 8, R), (GROUP - 1, 2, 8, R),
        (na, 8, 8, R), (nb, 8, 8, R), (na, 8, 8, R), (nb, 8, 8, R), (7, na, 8, R), (7, nb, 8, R),
        (COUNT, 8, R), (LEVELS - 1, COUNT, 8, R), (LEVELS - 1, COUNT, 8, R),
        (LEVELS - 1, R + 8, R), (LEVELS - 1, R + 8, R), (COUNT, R, R), (LEVELS, R, R),
        (LEVELS - 1, LEVEL_COLUMNS, R, R), (LEVELS - 1, LEVELS, R, R), ((LEVELS - 1) * R, 2 * R), (R, R),
        (STEP * STEP + 8, R), (STEP + 8, R), (8, R),
    ]
    dma = pltpu.SemaphoreType.DMA
    scratch = [pltpu.VMEM(shape, F32) for shape in shapes]
    scratch += [
        dma((5, leaves)), dma((leaves,)), dma((6,)), dma((6,)), dma((LEVELS - 1,)), dma((LEVELS - 1,)),
        dma((len(SWAPS),)), dma((len(SWAPS),)), dma((len(GATHERS),)), dma((len(GATHERS),)),
    ]
    solution, log_total = pl.pallas_call(
        kernel,
        out_shape=(
            jax.ShapeDtypeStruct((rows, R), F32),
            jax.ShapeDtypeStruct((1, 1), F32),
        ),
        in_specs=[any_spec] * 3,
        out_specs=(any_spec, pl.BlockSpec(memory_space=pltpu.SMEM)),
        scratch_shapes=scratch,
        compiler_params=pltpu.CompilerParams(
            collective_id=0, has_side_effects=True, vmem_limit_bytes=60 * 2**20
        ),
    )(leaf_inverse, bases, right_sides)
    return solution, log_total.reshape(())


def solution(mesh):
    return jax.shard_map(
        body,
        mesh=mesh,
        in_specs=(P("leaf", None, None), P("leaf", None, None), P("leaf", None)),
        out_specs=(P("leaf", None), P()),
        check_vma=False,
    )
```

time: 519 us -> 92.1 us (0.18); the launches traced: 514 us -> 91.9 us
  waiting for transfers between devices: 138 us -> 0 us
  other arithmetic: 118 us -> 0 us
  Pallas kernels: 0 us -> 87.4 us
  blocking collectives: 85.2 us -> 0 us
  matrix products: 81.3 us -> 0 us
  starting transfers between devices: 57.4 us -> 0 us
  local copies, waits for them, and re-layouts: 27.3 us -> 2.26 us
    ppermute x30 -> x0, waiting for transfers between devices: 138 us -> none  [swapped(): return lax.ppermute(value, axis, pairs)]
    another operation x25 -> x0, other arithmetic: 114 us -> none  [the longest x15 61.9 us: body(): factor = jnp.linalg.cholesky(capacity)]
    pallas_call x0 -> x1, Pallas kernels: none -> 87.4 us  [body(): pl.pallas_call(kernel, out_shape=(jax.ShapeDtypeStruct((rows, R), F32), j...]
    psum x1 -> x0, blocking collectives: 85.2 us -> none  [body(): total_log = lax.psum(log_share, 'leaf')]
    dot_general x11 -> x0, matrix products: 77.8 us -> none  [the longest x5 42.7 us: body(): jnp.einsum('ir,ic->rc', basis, current, precision=lax.Precision.HIGHEST)]
    ppermute x30 -> x0, starting transfers between devices: 57.4 us -> none  [swapped(): return lax.ppermute(value, axis, pairs)]
    concatenate x2 -> x0, local copies, waits for them, and re-layouts: 17.1 us -> none  [body(): jnp.concatenate([node_bases.reshape(row_count, level_count * rank_size),...]
    gather x5 -> x0, local copies, waits for them, and re-layouts: 6.22 us -> none  [body(): jnp.diagonal(factor)]
  transfers between devices with their start and end apart: 30 -> 0, of which waited for: 28 -> 0; matrix products, arithmetic and copies ran while one was open for 1% -> 0% of each run, Pallas kernels for 0% -> 0%
where the time goes in v2:
time: 92.1 us; the launch traced here: 91.9 us
  Pallas kernels  87.4 us (95%)
  between operations  2.33 us (3%)
  local copies, waits for them, and re-layouts  2.26 us (2%)
    pallas_call x1, Pallas kernels, body(): pl.pallas_call(kernel, out_shape=(jax.ShapeDtypeStruct((rows, R), F32), j...  87.4 us
    unnamed x1, local copies, waits for them, and re-layouts  2.26 us

profile of v2, /device:TPU:1, one launch (start us, length us, event | category | flops | bytes accessed | tf_op | source)
XLA Modules:
  0.0 91.9 jit_solution(4188424903432730498)
XLA Ops:
  0.6 87.4 %shard_map.50 = (f32[2048,128]{1,0:T(8,128)}, f32[1,1]{1,0:T(1,128)}) custom-call(f32[8,256,256]{2,1,0:T(8,128)} %d_hbm.1, f32[5,2048,128]{2,1,0:T(8,128)} %bitcast.2, f32[2048,128]{1,0:T(8,128)} %b_hbm.1), custom_call_target="tpu_custom_call" | custom-call | tf_op jit(solution)/shard_map/pallas_call | solution.py:516
  88.0 2.3 %copy.7 = f32[2048,128]{1,0:T(8,128)} copy(f32[2048,128]{1,0:T(8,128)} %get-tuple-element.8) | data formatting | bytes 2097152

commit v3 on v2

--- a/solution.py
+++ b/solution.py
@@ -22,10 +22,10 @@
     (0, 4), (0, 5), (1, 4), (1, 5), (2, 4), (2, 5), (3, 4), (4, 4), (3, 5), (4, 5),
 )
 COUNT = len(ORDER)
-A, B, END = 3, 10, COUNT
+A, B = (5, 10), (12, 20)
 GATHERS = {
-    "d0": (0, 1), "c0": (1, 3), "a0": (3, 5), "b0": (10, 12), "a1": (5, 8), "b1": (12, 14),
-    "a2": (8, 10), "b2": (14, 16), "b3": (16, 19), "b4": (19, 20),
+    "d0": (0, 1), "c0": (1, 3), "a0": (3, 5), "b0": (10, 12), "a1": (5, 7), "e1": (7, 8), "b1": (12, 14),
+    "a2": (8, 10), "b2": (14, 16), "b3": (16, 18), "e3": (18, 19), "b4": (19, 20),
 }
 SWAPS = {"a1": (5, 10), "b1": (12, 20), "a2": (8, 10), "b2": (14, 20), "b3": (16, 20), "b4": (19, 20)}
 GATHER_SLOT = {name: i for i, name in enumerate(GATHERS)}
@@ -131,7 +131,7 @@
 
 def kernel(
     d_hbm, u_hbm, b_hbm, o_hbm, total_ref,
-    dv, uv, bv, xv, ov, ab, g, rd, rs, ra, rb, ha, hb, qa, qb,
+    dv, uv, bv, xv, ov, ab, g, rd, rs, rta, rtb, ra, rb, ha, hb, qa, qb,
     pc, sx, rx, dx, dr, f, iv, tv, gt, zv, a_ref, column_ref, q_ref, log_ref,
     load_sem, out_sem, rs_send, rs_recv, d_send, d_recv, x_send, x_recv, g_send, g_recv,
 ):
@@ -199,36 +199,28 @@
             device_id=(who,), device_id_type=MESH,
         )
 
-    g[...] = jnp.zeros((COUNT, 8, 2, 8, R), F32)
-
-    def columns_of(leaf, columns):
+    def columns_of(columns):
         top = min(columns[-1], LEVELS - 1)
-        u = [uv[j, rows_of(leaf), :] for j in range(top + 1)]
-        have = [u[k] if k < LEVELS else bv[rows_of(leaf), :] for k in columns]
-        got = dot3(dv[leaf], jnp.concatenate(have, axis=1))
+        u = [uv[j] for j in range(top + 1)]
+        have = [u[k] if k < LEVELS else bv[...] for k in columns]
+        high, low = halves(jnp.concatenate(have, axis=1))
+        got = []
+        for leaf in range(leaves):
+            at = slice(size * leaf, size * (leaf + 1))
+            d_high, d_low = halves(dv[leaf])
+            got.append(
+                jnp.dot(
+                    jnp.concatenate([d_high, d_high, d_low], axis=1),
+                    jnp.concatenate([high[at], low[at], high[at]], axis=0),
+                    preferred_element_type=F32,
+                )
+            )
+        got = jnp.concatenate(got, axis=0)
         products = tdot3(jnp.concatenate(u, axis=1), got)
         for i, k in enumerate(columns):
-            xv[k, rows_of(leaf), :] = got[:, R * i : R * (i + 1)]
+            xv[k] = got[:, R * i : R * (i + 1)]
             for j in range(min(k, LEVELS - 1) + 1):
-                at = block(j, k)
-                g[at] = g[at] + products[R * j : R * (j + 1), R * i : R * (i + 1)].reshape(8, 2, 8, R)
-
-    def leaf_first(leaf, carry):
-        load_d(leaf).wait()
-        load_u(leaf, 0, 2, 1).wait()
-        columns_of(leaf, (0, 1))
-        return carry
-
-    def leaf_second(leaf, carry):
-        load_u(leaf, 2, 2, 2).wait()
-        columns_of(leaf, (2, 3))
-        return carry
-
-    def leaf_third(leaf, carry):
-        load_u(leaf, 4, 1, 3).wait()
-        load_b(leaf).wait()
-        columns_of(leaf, (4, 5))
-        return carry
+                g[block(j, k)] = products[R * j : R * (j + 1), R * i : R * (i + 1)].reshape(8, 2, 8, R)
 
     def scatter(first, count, target, slot):
         def one(r, carry):
@@ -248,36 +240,39 @@
             kept = kept + target[r]
         pc[pl.ds(first, count)] = kept
 
-    def to_mate(first, count, target, slot):
+    def to_mate(blocks, target, slot):
+        first, last = blocks
         return remote(
-            g.at[pl.ds(first, count), pl.ds(0, 8), 1 - core], target, rs_send.at[slot], rs_recv.at[slot], mate
+            g.at[pl.ds(first, last - first), pl.ds(0, 8), 1 - core], target, rs_send.at[slot], rs_recv.at[slot], mate
         )
 
-    def scatter_chips(first, count, from_mate, summed, target, slot):
-        to_mate(first, count, from_mate, slot - 1).wait_recv()
+    def scatter_chips(blocks, from_mate, summed, target, slot):
+        first, last = blocks
+        to_mate(blocks, from_mate, slot - 1).wait_recv()
 
         def add(i, carry):
             summed[i] = g[i + first, :, core] + from_mate[i]
             return carry
 
-        lax.fori_loop(0, count, add, 0)
+        lax.fori_loop(0, last - first, add, 0)
 
         def one(r, carry):
             other = (chip + r) % 8
             remote(
-                summed.at[pl.ds(0, count), other], target.at[r - 1],
+                summed.at[pl.ds(0, last - first), other], target.at[r - 1],
                 rs_send.at[slot], rs_recv.at[slot], device(other * 2 + core),
             ).start()
             return carry
 
         lax.fori_loop(1, 8, one, 0)
 
-    def scattered_chips(first, count, summed, target, slot):
+    def scattered_chips(blocks, summed, target, slot):
+        first, last = blocks
         remote(target, target, rs_send.at[slot], rs_recv.at[slot], me).wait_recv()
         kept = summed[:, chip]
         for r in range(7):
             kept = kept + target[r]
-        pc[pl.ds(first, count)] = kept
+        pc[pl.ds(first, last - first)] = kept
 
     def gather(name):
         first, last = GATHERS[name]
@@ -311,14 +306,17 @@
         at = pl.ds(first, last - first)
         return remote(sx.at[e - 1, at], rx.at[e - 1, at], x_send.at[slot], x_recv.at[slot], partner[e])
 
+    def whole(a, b):
+        return f[block(a, b)]
+
     def turn(level, k):
-        gt[level, k] = f[block(level, k)].T
+        gt[level, k] = whole(level, k).T
 
     def critical(level):
         e = level + 1
-        ratio = dot_full(iv[level], f[block(level, e)])
+        ratio = dot_full(iv[level], whole(level, e))
         tv[level, e] = ratio
-        dx[e - 1, pl.ds(0, R), :] = f[block(e, e)] - dot_full(gt[level, e], ratio)
+        dx[e - 1, pl.ds(0, R), :] = whole(e, e) - dot_full(gt[level, e], ratio)
         dx[e - 1, pl.ds(R, 8), :] = log_ref[...]
         diagonal(e).start()
 
@@ -326,27 +324,28 @@
         e = level + 1
         first, last = SWAPS[name]
         fresh = [k for k in columns if k != e]
-        ratio = dot_full(iv[level], jnp.concatenate([f[block(level, k)] for k in fresh], axis=1))
+        ratio = dot3(iv[level], jnp.concatenate([whole(level, k) for k in fresh], axis=1))
         for i, k in enumerate(fresh):
             tv[level, k] = ratio[:, R * i : R * (i + 1)]
             if k < LEVELS:
                 turn(level, k)
         ends = [r for r in range(e, LEVELS) if r <= columns[-1]]
         left = jnp.concatenate([gt[level, r, pl.ds(piece, 8), :] for r in ends], axis=0)
-        down = dot_full(left, ratio)
+        down = dot3(left, ratio)
         for at in range(first, last):
             r, k = ORDER[at]
             i = fresh.index(k)
             sx[e - 1, at] = pc[at] - down[8 * (r - e) : 8 * (r - e) + 8, R * i : R * (i + 1)]
         swap(name).start()
 
-    def merge(name):
+    def merge(name, *sets):
         first, last = SWAPS[name]
         e = int(name[1])
         swap(name).wait_recv()
         at = pl.ds(first, last - first)
         pc[at] = sx[e - 1, at] + rx[e - 1, at]
-        gather(name)
+        for each in sets:
+            gather(each)
 
     def enter(e):
         diagonal(e).wait_recv()
@@ -361,123 +360,138 @@
         lax.broadcasted_iota(jnp.int32, (R, R), 0) == lax.broadcasted_iota(jnp.int32, (R, R), 1)
     ).astype(F32)
 
-    lax.fori_loop(0, leaves, leaf_first, 0)
+    for leaf in range(leaves):
+        load_d(leaf).wait()
+        load_u(leaf, 0, 2, 1).wait()
+    columns_of((0, 1))
     pl.semaphore_wait(barrier, GROUP - 1 + LEVELS - 1)
     scatter(0, 1, rd, 0)
     scatter(1, 2, rs, 1)
-    lax.fori_loop(0, leaves, leaf_second, 0)
+    for leaf in range(leaves):
+        load_u(leaf, 2, 2, 2).wait()
+    columns_of((2, 3))
+    scatter(3, 2, rta, 2)
+    to_mate(A, ra, 4).start()
     scattered(0, 1, rd, 0)
     gather("d0")
-    to_mate(A, B - A, ra, 2).start()
-    lax.fori_loop(0, leaves, leaf_third, 0)
-    to_mate(B, END - B, rb, 4).start()
+    for leaf in range(leaves):
+        load_u(leaf, 4, 1, 3).wait()
+        load_b(leaf).wait()
+    columns_of((4, 5))
+    scatter(10, 2, rtb, 3)
+    to_mate(B, rb, 6).start()
     scattered(1, 2, rs, 1)
     gather("c0")
-    scatter_chips(A, B - A, ra, ha, qa, 3)
+    scatter_chips(A, ra, ha, qa, 5)
     gathered("d0").wait_recv()
-    a_ref[...] = f[0] + eye
+    a_ref[...] = whole(0, 0) + eye
     log_ref[...] = jnp.zeros((8, R), F32)
 
-    def task_0():
-        scatter_chips(B, END - B, rb, hb, qb, 5)
-
-    invert(0, {4: task_0})
+    def task_0a():
+        scattered(3, 2, rta, 2)
+        gather("a0")
+
+    def task_0b():
+        scatter_chips(B, rb, hb, qb, 7)
+
+    def task_0c():
+        scattered(10, 2, rtb, 3)
+        gather("b0")
+
+    invert(0, {1: task_0a, 3: task_0b, 6: task_0c})
     gathered("c0").wait_recv()
     turn(0, 1)
     critical(0)
-    scattered_chips(A, B - A, ha, qa, 3)
-    gather("a0")
-    scattered_chips(B, END - B, hb, qb, 5)
-    gather("b0")
+    scattered_chips(A, ha, qa, 5)
     gathered("a0").wait_recv()
     lower(0, (2, 3), "a1")
 
     enter(1)
+    merge("a1", "a1", "e1")
 
     def task_1a():
-        merge("a1")
-
-    def task_1b():
+        scattered_chips(B, hb, qb, 7)
         gathered("b0").wait_recv()
         lower(0, (4, 5), "b1")
 
-    invert(1, {3: task_1a, 5: task_1b})
+    def task_1b():
+        merge("b1", "b1")
+
+    invert(1, {1: task_1a, 5: task_1b})
     gathered("a1").wait_recv()
     turn(1, 2)
     critical(1)
+    gathered("e1").wait_recv()
     lower(1, (2, 3), "a2")
-    merge("b1")
 
     enter(2)
-    merge("a2")
+    merge("a2", "a2")
 
     def task_2a():
         gathered("b1").wait_recv()
         lower(1, (4, 5), "b2")
 
     def task_2b():
-        merge("b2")
-
-    invert(2, {2: task_2a, 6: task_2b})
+        merge("b2", "b2")
+
+    invert(2, {1: task_2a, 5: task_2b})
     gathered("a2").wait_recv()
     turn(2, 3)
     critical(2)
-
     gathered("b2").wait_recv()
     lower(2, (4, 5), "b3")
+
     enter(3)
 
     def task_3():
-        merge("b3")
-
-    invert(3, {3: task_3})
+        merge("b3", "b3", "e3")
+
+    invert(3, {2: task_3})
     gathered("b3").wait_recv()
     turn(3, 4)
     critical(3)
+    gathered("e3").wait_recv()
     lower(3, (4, 5), "b4")
 
     for level in range(LEVELS - 2, -1, -1):
         pair = jnp.concatenate([tv[level, 4], tv[level, 5]], axis=1)
         if level < LEVELS - 2:
             between = jnp.concatenate([tv[level, k] for k in range(level + 1, LEVELS - 1)], axis=1)
-            pair = pair - dot_full(between, zv[pl.ds(R * (level + 1), R * (LEVELS - 2 - level)), :])
+            pair = pair - dot3(between, zv[pl.ds(R * (level + 1), R * (LEVELS - 2 - level)), :])
         zv[pl.ds(R * level, R), :] = pair
     z_high, z_low = halves(zv[...])
     z_stack = jnp.concatenate([z_high, z_low, z_high], axis=0)
 
-    def update(leaf, carry):
-        high, low = halves(jnp.concatenate([xv[k, rows_of(leaf), :] for k in range(LEVELS - 1)], axis=1))
-        change = jnp.dot(jnp.concatenate([high, high, low], axis=1), z_stack, preferred_element_type=F32)
-        ab[rows_of(leaf), :] = jnp.concatenate([xv[k, rows_of(leaf), :] for k in (4, 5)], axis=1) - change
-        return carry
-
-    lax.fori_loop(0, leaves, update, 0)
-
-    merge("b4")
+    high, low = halves(jnp.concatenate([xv[k] for k in range(LEVELS - 1)], axis=1))
+    change = jnp.dot(jnp.concatenate([high, high, low], axis=1), z_stack, preferred_element_type=F32)
+    ab[...] = jnp.concatenate([xv[k] for k in (4, 5)], axis=1) - change
+
+    merge("b4", "b4")
     enter(4)
     invert(4, {})
     gathered("b4").wait_recv()
-    weights = dot_full(iv[4], f[block(4, 5)])
+    weights = dot_full(iv[4], whole(4, 5))
     w_high, w_low = halves(weights)
     w_stack = jnp.concatenate([w_high, w_low, w_high], axis=0)
 
-    def store(leaf):
-        return pltpu.make_async_copy(ov.at[rows_of(leaf), :], o_hbm.at[rows_of(leaf), :], out_sem.at[leaf])
-
-    def last(leaf, carry):
-        high, low = halves(ab[rows_of(leaf), pl.ds(0, R)])
+    part = 2 * size
+
+    def store(i):
+        at = pl.ds(i * part, part)
+        return pltpu.make_async_copy(ov.at[at, :], o_hbm.at[at, :], out_sem.at[i])
+
+    for i in range(leaves // 2):
+        at = pl.ds(i * part, part)
+        high, low = halves(ab[at, pl.ds(0, R)])
         change = jnp.dot(jnp.concatenate([high, high, low], axis=1), w_stack, preferred_element_type=F32)
-        ov[rows_of(leaf), :] = ab[rows_of(leaf), pl.ds(R, R)] - change
-        store(leaf).start()
-        return carry
-
-    lax.fori_loop(0, leaves, last, 0)
+        ov[at, :] = ab[at, pl.ds(R, R)] - change
+        store(i).start()
     total_ref[0, 0] = jnp.sum(log_ref[...]) / (R * R * (2**LEVELS - 1))
 
-    for target, slot in ((rd, 0), (rs, 1), (qa, 3), (qb, 5)):
+    for target, slot in ((rd, 0), (rs, 1), (rta, 2), (rtb, 3), (qa, 5), (qb, 7)):
         remote(target, target, rs_send.at[slot], rs_recv.at[slot], me).wait_send()
-    to_mate(A, B - A, ra, 2).wait_send()
-    to_mate(B, END - B, rb, 4).wait_send()
+    to_mate(A, ra, 4).wait_send()
+    to_mate(B, rb, 6).wait_send()
     for name in GATHERS:
         gathered(name).wait_send()
     for name in SWAPS:
@@ -485,11 +499,8 @@
     for e in range(1, LEVELS):
         diagonal(e).wait_send()
 
-    def finish(leaf, carry):
-        store(leaf).wait()
-        return carry
-
-    lax.fori_loop(0, leaves, finish, 0)
+    for i in range(leaves // 2):
+        store(i).wait()
 
 
 def body(leaf_inverse, node_bases, right_sides):
@@ -497,10 +508,10 @@
     rows = right_sides.shape[0]
     bases = jnp.transpose(node_bases, (1, 0, 2))
     any_spec = pl.BlockSpec(memory_space=pl.ANY)
-    na, nb = B - A, END - B
+    na, nb = A[1] - A[0], B[1] - B[0]
     shapes = [
         (leaves, size, size), (LEVELS, rows, R), (rows, R), (LEVEL_COLUMNS, rows, R), (rows, R), (rows, 2 * R),
-        (COUNT, 8, 2, 8, R), (GROUP - 1, 1, 8, R), (GROUP - 1, 2, 8, R),
+        (COUNT, 8, 2, 8, R), (GROUP - 1, 1, 8, R), (GROUP - 1, 2, 8, R), (GROUP - 1, 2, 8, R), (GROUP - 1, 2, 8, R),
         (na, 8, 8, R), (nb, 8, 8, R), (na, 8, 8, R), (nb, 8, 8, R), (7, na, 8, R), (7, nb, 8, R),
         (COUNT, 8, R), (LEVELS - 1, COUNT, 8, R), (LEVELS - 1, COUNT, 8, R),
         (LEVELS - 1, R + 8, R), (LEVELS - 1, R + 8, R), (COUNT, R, R), (LEVELS, R, R),
@@ -510,7 +521,7 @@
     dma = pltpu.SemaphoreType.DMA
     scratch = [pltpu.VMEM(shape, F32) for shape in shapes]
     scratch += [
-        dma((5, leaves)), dma((leaves,)), dma((6,)), dma((6,)), dma((LEVELS - 1,)), dma((LEVELS - 1,)),
+        dma((5, leaves)), dma((leaves,)), dma((8,)), dma((8,)), dma((LEVELS - 1,)), dma((LEVELS - 1,)),
         dma((len(SWAPS),)), dma((len(SWAPS),)), dma((len(GATHERS),)), dma((len(GATHERS),)),
     ]
     solution, log_total = pl.pallas_call(

time: 92.1 us -> 82.6 us (0.90)
  Pallas kernels: 87.4 us -> 77.8 us
    pallas_call x1, Pallas kernels: 87.4 us -> 77.8 us  [body(): pl.pallas_call(kernel, out_shape=(jax.ShapeDtypeStruct((rows, R), F32), j...]
where the time goes in v3:
time: 82.6 us; the launch traced here: 82.4 us
  Pallas kernels  77.8 us (94%)
  between operations  2.33 us (3%)
  local copies, waits for them, and re-layouts  2.26 us (3%)
    pallas_call x1, Pallas kernels, body(): pl.pallas_call(kernel, out_shape=(jax.ShapeDtypeStruct((rows, R), F32), j...  77.8 us
    unnamed x1, local copies, waits for them, and re-layouts  2.26 us

profile of v3, /device:TPU:1, one launch (start us, length us, event | category | flops | bytes accessed | tf_op | source)
XLA Modules:
  0.0 82.4 jit_solution(502638225008424465)
XLA Ops:
  0.6 77.8 %shard_map.50 = (f32[2048,128]{1,0:T(8,128)}, f32[1,1]{1,0:T(1,128)}) custom-call(f32[8,256,256]{2,1,0:T(8,128)} %d_hbm.1, f32[5,2048,128]{2,1,0:T(8,128)} %bitcast.2, f32[2048,128]{1,0:T(8,128)} %b_hbm.1), custom_call_target="tpu_custom_call" | custom-call | tf_op jit(solution)/shard_map/pallas_call | solution.py:527
  78.5 2.3 %copy.7 = f32[2048,128]{1,0:T(8,128)} copy(f32[2048,128]{1,0:T(8,128)} %get-tuple-element.8) | data formatting | bytes 2097152

commit v4 on v3

--- a/solution.py
+++ b/solution.py
@@ -130,8 +130,8 @@
 
 
 def kernel(
-    d_hbm, u_hbm, b_hbm, o_hbm, total_ref,
-    dv, uv, bv, xv, ov, ab, g, rd, rs, rta, rtb, ra, rb, ha, hb, qa, qb,
+    d_hbm, u_hbm, b_hbm, ab_hbm, weights_ref, total_ref,
+    dv, uv, bv, xv, ab, g, rd, rs, rta, rtb, ra, rb, ha, hb, qa, qb,
     pc, sx, rx, dx, dr, f, iv, tv, gt, zv, a_ref, column_ref, q_ref, log_ref,
     load_sem, out_sem, rs_send, rs_recv, d_send, d_recv, x_send, x_recv, g_send, g_recv,
 ):
@@ -231,7 +231,7 @@
             ).start()
             return carry
 
-        lax.fori_loop(1, GROUP, one, 0)
+        lax.fori_loop(1, GROUP, one, 0, unroll=3)
 
     def scattered(first, count, target, slot):
         remote(target, target, rs_send.at[slot], rs_recv.at[slot], me).wait_recv()
@@ -264,7 +264,7 @@
             ).start()
             return carry
 
-        lax.fori_loop(1, 8, one, 0)
+        lax.fori_loop(1, 8, one, 0, unroll=True)
 
     def scattered_chips(blocks, summed, target, slot):
         first, last = blocks
@@ -288,7 +288,7 @@
             ).start()
             return carry
 
-        lax.fori_loop(1, GROUP, one, 0)
+        lax.fori_loop(1, GROUP, one, 0, unroll=3)
 
     def gathered(name):
         first, last = GATHERS[name]
@@ -398,43 +398,39 @@
         scattered(10, 2, rtb, 3)
         gather("b0")
 
-    invert(0, {1: task_0a, 3: task_0b, 6: task_0c})
+    invert(0, {1: task_0a, 3: task_0b, 5: task_0c})
     gathered("c0").wait_recv()
     turn(0, 1)
     critical(0)
     scattered_chips(A, ha, qa, 5)
     gathered("a0").wait_recv()
     lower(0, (2, 3), "a1")
+    scattered_chips(B, hb, qb, 7)
+    gathered("b0").wait_recv()
+    lower(0, (4, 5), "b1")
 
     enter(1)
     merge("a1", "a1", "e1")
 
-    def task_1a():
-        scattered_chips(B, hb, qb, 7)
-        gathered("b0").wait_recv()
-        lower(0, (4, 5), "b1")
-
-    def task_1b():
+    def task_1():
         merge("b1", "b1")
 
-    invert(1, {1: task_1a, 5: task_1b})
+    invert(1, {3: task_1})
     gathered("a1").wait_recv()
     turn(1, 2)
     critical(1)
     gathered("e1").wait_recv()
     lower(1, (2, 3), "a2")
+    gathered("b1").wait_recv()
+    lower(1, (4, 5), "b2")
 
     enter(2)
     merge("a2", "a2")
 
-    def task_2a():
-        gathered("b1").wait_recv()
-        lower(1, (4, 5), "b2")
-
-    def task_2b():
+    def task_2():
         merge("b2", "b2")
 
-    invert(2, {1: task_2a, 5: task_2b})
+    invert(2, {3: task_2})
     gathered("a2").wait_recv()
     turn(2, 3)
     critical(2)
@@ -442,11 +438,8 @@
     lower(2, (4, 5), "b3")
 
     enter(3)
-
-    def task_3():
-        merge("b3", "b3", "e3")
-
-    invert(3, {2: task_3})
+    merge("b3", "b3", "e3")
+    invert(3, {})
     gathered("b3").wait_recv()
     turn(3, 4)
     critical(3)
@@ -465,27 +458,14 @@
     high, low = halves(jnp.concatenate([xv[k] for k in range(LEVELS - 1)], axis=1))
     change = jnp.dot(jnp.concatenate([high, high, low], axis=1), z_stack, preferred_element_type=F32)
     ab[...] = jnp.concatenate([xv[k] for k in (4, 5)], axis=1) - change
+    leave = pltpu.make_async_copy(ab, ab_hbm, out_sem)
+    leave.start()
 
     merge("b4", "b4")
     enter(4)
     invert(4, {})
     gathered("b4").wait_recv()
-    weights = dot_full(iv[4], whole(4, 5))
-    w_high, w_low = halves(weights)
-    w_stack = jnp.concatenate([w_high, w_low, w_high], axis=0)
-
-    part = 2 * size
-
-    def store(i):
-        at = pl.ds(i * part, part)
-        return pltpu.make_async_copy(ov.at[at, :], o_hbm.at[at, :], out_sem.at[i])
-
-    for i in range(leaves // 2):
-        at = pl.ds(i * part, part)
-        high, low = halves(ab[at, pl.ds(0, R)])
-        change = jnp.dot(jnp.concatenate([high, high, low], axis=1), w_stack, preferred_element_type=F32)
-        ov[at, :] = ab[at, pl.ds(R, R)] - change
-        store(i).start()
+    weights_ref[...] = dot_full(iv[4], whole(4, 5))
     total_ref[0, 0] = jnp.sum(log_ref[...]) / (R * R * (2**LEVELS - 1))
 
     for target, slot in ((rd, 0), (rs, 1), (rta, 2), (rtb, 3), (qa, 5), (qb, 7)):
@@ -499,8 +479,15 @@
     for e in range(1, LEVELS):
         diagonal(e).wait_send()
 
-    for i in range(leaves // 2):
-        store(i).wait()
+    leave.wait()
+
+
+def finish(columns_ref, weights_ref, total_ref, o_ref, log_ref):
+    o_ref[...] = columns_ref[:, R:] - dot3(columns_ref[:, :R], weights_ref[...])
+
+    @pl.when(pl.program_id(0) == 0)
+    def _():
+        log_ref[0, 0] = total_ref[0, 0]
 
 
 def body(leaf_inverse, node_bases, right_sides):
@@ -510,7 +497,7 @@
     any_spec = pl.BlockSpec(memory_space=pl.ANY)
     na, nb = A[1] - A[0], B[1] - B[0]
     shapes = [
-        (leaves, size, size), (LEVELS, rows, R), (rows, R), (LEVEL_COLUMNS, rows, R), (rows, R), (rows, 2 * R),
+        (leaves, size, size), (LEVELS, rows, R), (rows, R), (LEVEL_COLUMNS, rows, R), (rows, 2 * R),
         (COUNT, 8, 2, 8, R), (GROUP - 1, 1, 8, R), (GROUP - 1, 2, 8, R), (GROUP - 1, 2, 8, R), (GROUP - 1, 2, 8, R),
         (na, 8, 8, R), (nb, 8, 8, R), (na, 8, 8, R), (nb, 8, 8, R), (7, na, 8, R), (7, nb, 8, R),
         (COUNT, 8, R), (LEVELS - 1, COUNT, 8, R), (LEVELS - 1, COUNT, 8, R),
@@ -521,22 +508,39 @@
     dma = pltpu.SemaphoreType.DMA
     scratch = [pltpu.VMEM(shape, F32) for shape in shapes]
     scratch += [
-        dma((5, leaves)), dma((leaves,)), dma((8,)), dma((8,)), dma((LEVELS - 1,)), dma((LEVELS - 1,)),
+        dma((5, leaves)), dma(()), dma((8,)), dma((8,)), dma((LEVELS - 1,)), dma((LEVELS - 1,)),
         dma((len(SWAPS),)), dma((len(SWAPS),)), dma((len(GATHERS),)), dma((len(GATHERS),)),
     ]
-    solution, log_total = pl.pallas_call(
+    smem = pl.BlockSpec(memory_space=pltpu.SMEM)
+    columns, weights, total = pl.pallas_call(
         kernel,
         out_shape=(
-            jax.ShapeDtypeStruct((rows, R), F32),
+            jax.ShapeDtypeStruct((rows, 2 * R), F32),
+            jax.ShapeDtypeStruct((R, R), F32),
             jax.ShapeDtypeStruct((1, 1), F32),
         ),
         in_specs=[any_spec] * 3,
-        out_specs=(any_spec, pl.BlockSpec(memory_space=pltpu.SMEM)),
+        out_specs=(any_spec, pl.BlockSpec(memory_space=pltpu.VMEM), smem),
         scratch_shapes=scratch,
         compiler_params=pltpu.CompilerParams(
             collective_id=0, has_side_effects=True, vmem_limit_bytes=60 * 2**20
         ),
     )(leaf_inverse, bases, right_sides)
+    part = rows // 4
+    solution, log_total = pl.pallas_call(
+        finish,
+        grid=(4,),
+        out_shape=(
+            jax.ShapeDtypeStruct((rows, R), F32),
+            jax.ShapeDtypeStruct((1, 1), F32),
+        ),
+        in_specs=[
+            pl.BlockSpec((part, 2 * R), lambda i: (i, 0)),
+            pl.BlockSpec((R, R), lambda i: (0, 0)),
+            smem,
+        ],
+        out_specs=(pl.BlockSpec((part, R), lambda i: (i, 0)), smem),
+    )(columns, weights, total)
     return solution, log_total.reshape(())
 
 

time: 82.6 us -> 79.6 us (0.964)
  local copies, waits for them, and re-layouts: 2.26 us -> 0 us
  between operations: 2.33 us -> 0.64 us
  Pallas kernels: 77.8 us -> 78.8 us
    unnamed x1 -> x0, local copies, waits for them, and re-layouts: 2.26 us -> none
    pallas_call x1 -> x2, Pallas kernels: 77.8 us -> 78.8 us  [the longest x1 74.2 us: body(): pl.pallas_call(kernel, out_shape=(jax.ShapeDtypeStruct((rows, 2 * R), F32...]
where the time goes in v4:
time: 79.6 us; the launch traced here: 79.5 us
  Pallas kernels  78.8 us (99%)
    pallas_call x1, Pallas kernels, body(): pl.pallas_call(kernel, out_shape=(jax.ShapeDtypeStruct((rows, 2 * R), F32...  74.2 us
    pallas_call x1, Pallas kernels, body(): pl.pallas_call(finish, grid=(4,), out_shape=(jax.ShapeDtypeStruct((rows,...  4.65 us

profile of v4, /device:TPU:1, one launch (start us, length us, event | category | flops | bytes accessed | tf_op | source)
XLA Modules:
  0.0 79.5 jit_solution(5253837688736240053)
XLA Ops:
  0.6 74.2 %shard_map.50 = (f32[2048,256]{1,0:T(8,128)}, f32[128,128]{1,0:T(8,128)}, f32[1,1]{1,0:T(1,128)}) custom-call(f32[8,256,256]{2,1,0:T(8,128)} %d_hbm.1, f32[5,2048,128]{2,1,0:T(8,128)} %bitcast.2, f32[2048,128]{1,0:T(8,128)} %b_hbm.1), custom_call_target="tpu_custom_call" | custom-call | tf_op jit(solution)/shard_map/pallas_call | solution.py:515
  74.8 4.6 %shard_map.51 = (f32[2048,128]{1,0:T(8,128)}, f32[1,1]{1,0:T(1,128)}) custom-call(f32[2048,256]{1,0:T(8,128)} %get-tuple-element.7.columns_ref, f32[128,128]{1,0:T(8,128)} %get-tuple-element.8.weights_ref, f32[1,1]{1,0:T(1,128)} %get-tuple-element.9.total_ref), custom_call_target="tpu_custom_call" | custom-call | tf_op jit(solution)/shard_map/pallas_call | solution.py:530

commit v5 on v4

--- a/solution.py
+++ b/solution.py
@@ -161,6 +161,22 @@
         me + 32 * (7 - 2 * z),
     )
 
+    def rows_of(leaf):
+        return pl.ds(pl.multiple_of(leaf * size, size), size)
+
+    def load_d(leaf):
+        return pltpu.make_async_copy(d_hbm.at[leaf], dv.at[leaf], load_sem.at[0, leaf])
+
+    def load_u(leaf, first, count, slot):
+        at = (pl.ds(first, count), rows_of(leaf), slice(None))
+        return pltpu.make_async_copy(u_hbm.at[at], uv.at[at], load_sem.at[slot, leaf])
+
+    def load_b(leaf):
+        return pltpu.make_async_copy(b_hbm.at[rows_of(leaf), :], bv.at[rows_of(leaf), :], load_sem.at[4, leaf])
+
+    for leaf in range(leaves):
+        load_d(leaf).start()
+        load_u(leaf, 0, 2, 1).start()
     barrier = pltpu.get_barrier_semaphore()
 
     def greet(r, carry):
@@ -171,22 +187,6 @@
     for e in range(1, LEVELS):
         pl.semaphore_signal(barrier, inc=1, device_id=(partner[e],), device_id_type=MESH)
 
-    def rows_of(leaf):
-        return pl.ds(pl.multiple_of(leaf * size, size), size)
-
-    def load_d(leaf):
-        return pltpu.make_async_copy(d_hbm.at[leaf], dv.at[leaf], load_sem.at[0, leaf])
-
-    def load_u(leaf, first, count, slot):
-        at = (pl.ds(first, count), rows_of(leaf), slice(None))
-        return pltpu.make_async_copy(u_hbm.at[at], uv.at[at], load_sem.at[slot, leaf])
-
-    def load_b(leaf):
-        return pltpu.make_async_copy(b_hbm.at[rows_of(leaf), :], bv.at[rows_of(leaf), :], load_sem.at[4, leaf])
-
-    for leaf in range(leaves):
-        load_d(leaf).start()
-        load_u(leaf, 0, 2, 1).start()
     for leaf in range(leaves):
         load_u(leaf, 2, 2, 2).start()
     for leaf in range(leaves):
@@ -231,7 +231,7 @@
             ).start()
             return carry
 
-        lax.fori_loop(1, GROUP, one, 0, unroll=3)
+        lax.fori_loop(1, GROUP, one, 0, unroll=5)
 
     def scattered(first, count, target, slot):
         remote(target, target, rs_send.at[slot], rs_recv.at[slot], me).wait_recv()
@@ -288,7 +288,7 @@
             ).start()
             return carry
 
-        lax.fori_loop(1, GROUP, one, 0, unroll=3)
+        lax.fori_loop(1, GROUP, one, 0, unroll=5)
 
     def gathered(name):
         first, last = GATHERS[name]
@@ -526,10 +526,10 @@
             collective_id=0, has_side_effects=True, vmem_limit_bytes=60 * 2**20
         ),
     )(leaf_inverse, bases, right_sides)
-    part = rows // 4
+    part = rows // 2
     solution, log_total = pl.pallas_call(
         finish,
-        grid=(4,),
+        grid=(2,),
         out_shape=(
             jax.ShapeDtypeStruct((rows, R), F32),
             jax.ShapeDtypeStruct((1, 1), F32),

time: 79.6 us -> 77.8 us (0.977)
  Pallas kernels: 78.8 us -> 77 us
    pallas_call x1, Pallas kernels: 4.65 us -> 3.36 us  [body(): pl.pallas_call(finish, grid=(2,), out_shape=(jax.ShapeDtypeStruct((rows,...]
where the time goes in v5:
time: 77.8 us; the launch traced here: 77.6 us
  Pallas kernels  77 us (99%)
    pallas_call x1, Pallas kernels, body(): pl.pallas_call(kernel, out_shape=(jax.ShapeDtypeStruct((rows, 2 * R), F32...  73.6 us
    pallas_call x1, Pallas kernels, body(): pl.pallas_call(finish, grid=(2,), out_shape=(jax.ShapeDtypeStruct((rows,...  3.36 us

profile of v5, /device:TPU:1, one launch (start us, length us, event | category | flops | bytes accessed | tf_op | source)
XLA Modules:
  0.0 77.6 jit_solution(18094378147826733157)
XLA Ops:
  0.6 73.6 %shard_map.50 = (f32[2048,256]{1,0:T(8,128)}, f32[128,128]{1,0:T(8,128)}, f32[1,1]{1,0:T(1,128)}) custom-call(f32[8,256,256]{2,1,0:T(8,128)} %d_hbm.1, f32[5,2048,128]{2,1,0:T(8,128)} %bitcast.2, f32[2048,128]{1,0:T(8,128)} %b_hbm.1), custom_call_target="tpu_custom_call" | custom-call | tf_op jit(solution)/shard_map/pallas_call | solution.py:515
  74.3 3.4 %shard_map.51 = (f32[2048,128]{1,0:T(8,128)}, f32[1,1]{1,0:T(1,128)}) custom-call(f32[2048,256]{1,0:T(8,128)} %get-tuple-element.7.columns_ref, f32[128,128]{1,0:T(8,128)} %get-tuple-element.8.weights_ref, f32[1,1]{1,0:T(1,128)} %get-tuple-element.9.total_ref), custom_call_target="tpu_custom_call" | custom-call | tf_op jit(solution)/shard_map/pallas_call | solution.py:530

commit v6 on v5

--- a/solution.py
+++ b/solution.py
@@ -398,7 +398,7 @@
         scattered(10, 2, rtb, 3)
         gather("b0")
 
-    invert(0, {1: task_0a, 3: task_0b, 5: task_0c})
+    invert(0, {1: task_0a, 2: task_0b, 4: task_0c})
     gathered("c0").wait_recv()
     turn(0, 1)
     critical(0)

time: 77.8 us -> 77.8 us (level)
  no operation moved by 1% of the time
where the time goes in v6:
time: 77.8 us; the launch traced here: 77.6 us
  Pallas kernels  77 us (99%)
    pallas_call x1, Pallas kernels, body(): pl.pallas_call(kernel, out_shape=(jax.ShapeDtypeStruct((rows, 2 * R), F32...  73.6 us
    pallas_call x1, Pallas kernels, body(): pl.pallas_call(finish, grid=(2,), out_shape=(jax.ShapeDtypeStruct((rows,...  3.36 us

profile of v6, /device:TPU:1, one launch (start us, length us, event | category | flops | bytes accessed | tf_op | source)
XLA Modules:
  0.0 77.6 jit_solution(1374402452206915682)
XLA Ops:
  0.6 73.6 %shard_map.50 = (f32[2048,256]{1,0:T(8,128)}, f32[128,128]{1,0:T(8,128)}, f32[1,1]{1,0:T(1,128)}) custom-call(f32[8,256,256]{2,1,0:T(8,128)} %d_hbm.1, f32[5,2048,128]{2,1,0:T(8,128)} %bitcast.2, f32[2048,128]{1,0:T(8,128)} %b_hbm.1), custom_call_target="tpu_custom_call" | custom-call | tf_op jit(solution)/shard_map/pallas_call | solution.py:515
  74.3 3.4 %shard_map.51 = (f32[2048,128]{1,0:T(8,128)}, f32[1,1]{1,0:T(1,128)}) custom-call(f32[2048,256]{1,0:T(8,128)} %get-tuple-element.7.columns_ref, f32[128,128]{1,0:T(8,128)} %get-tuple-element.8.weights_ref, f32[1,1]{1,0:T(1,128)} %get-tuple-element.9.total_ref), custom_call_target="tpu_custom_call" | custom-call | tf_op jit(solution)/shard_map/pallas_call | solution.py:530
